TPU v7x, 32 devices: a whole 2x2x4 slice. The times are simulated.
32 devices in a mesh: dp: 8 (over z, x), tensor: 4 (over y, core).
Axes of the slice: x: 2, y: 2, z: 4, core: 2. Of those that a mesh axis runs over, the one named last changes fastest.
Arguments:
- inputs: bfloat16 [16, 512, 2048], P('dp', 'tensor'), may hold values from -6 to 6
- query_weight: bfloat16 [2048, 2048], P('dp', 'tensor'), may hold values from -0.125 to 0.125
- key_weight: bfloat16 [2048, 2048], P('dp', 'tensor'), may hold values from -0.125 to 0.125
- value_weight: bfloat16 [2048, 2048], P('dp', 'tensor'), may hold values from -0.125 to 0.125
- out_weight: bfloat16 [2048, 2048], P('dp', 'tensor'), may hold values from -0.125 to 0.125
- query_gain: float32 [2048], P('tensor'), may hold values from 0.25 to 1.75
- key_gain: float32 [2048], P('tensor'), may hold values from 0.25 to 1.75
- attn_gain: float32 [2048], replicated, may hold values from 0.25 to 1.75
- gate_weight: bfloat16 [2048, 8192], P('dp', 'tensor'), may hold values from -0.125 to 0.125
- up_weight: bfloat16 [2048, 8192], P('dp', 'tensor'), may hold values from -0.125 to 0.125
- down_weight: bfloat16 [2048, 8192], P('dp', 'tensor'), may hold values from -0.0625 to 0.0625
- ffn_gain: float32 [2048], replicated, may hold values from 0.25 to 1.75
- positions: int32 [16, 512], P('dp'), may hold values from 0 to 1023, as said below
- block_ids: int32 [16, 512], P('dp'), may hold values from 0 to 3, never falling along the last dimension, each value on 1 to 256 neighbouring positions
- cotangent: float32 [16, 512, 2048], P('dp', 'tensor'), may hold values from -6 to 6
Outputs:
- output: bfloat16 [16, 512, 2048], P('dp', 'tensor')
- input_grad: float32 [16, 512, 2048], P('dp', 'tensor')
- query_grad: float32 [2048, 2048], P('dp', 'tensor')
- key_grad: float32 [2048, 2048], P('dp', 'tensor')
- value_grad: float32 [2048, 2048], P('dp', 'tensor')
- out_grad: float32 [2048, 2048], P('dp', 'tensor')
- query_gain_grad: float32 [2048], P('tensor')
- key_gain_grad: float32 [2048], P('tensor')
- attn_gain_grad: float32 [2048], replicated
- gate_grad: float32 [2048, 8192], P('dp', 'tensor')
- up_grad: float32 [2048, 8192], P('dp', 'tensor')
- down_grad: float32 [2048, 8192], P('dp', 'tensor')
- ffn_gain_grad: float32 [2048], replicated
Inputs may be any that keep to these rules, and one draw needn't show every extreme that they name: `positions`: positions rise strictly along each sequence; the first is 0 and the last 1023. `block_ids`: block ids never fall along a sequence and a block holds at most 256 positions.
All inputs are finite; a program needn't handle non-finite values.
Results may differ from a plain program's by a relative error of at most 0.02.
Values may be sent and summed in bfloat16 or wider, within the bound.
A program may use at most 256 MiB of HBM per device.

v0:
```python
import jax
import jax.numpy as jnp
from jax import lax
from jax.sharding import PartitionSpec as P

D = 2048
HD = 128


EPS = 1e-06
THETA = 500000.0
NEG_FILL = -1e30


def rope_tables(position_ids):
    inv_freq = 1.0 / THETA ** (jnp.arange(0, HD, 2, dtype=jnp.float32) / HD)
    angles = position_ids.astype(jnp.float32)[:, None] * inv_freq[None, :]
    angles = jnp.concatenate([angles, angles], axis=1)
    return (jnp.cos(angles), jnp.sin(angles))


def turn_heads(values, cosine, sine):
    half_width = values.shape[-1] // 2
    rotated = jnp.concatenate([-values[..., half_width:], values[..., :half_width]], axis=-1)
    return values * cosine[:, None, :] + rotated * sine[:, None, :]


def turn_back(grads, cosine, sine):
    half_width = grads.shape[-1] // 2
    scaled = grads * sine[:, None, :]
    moved_part = jnp.concatenate([scaled[..., half_width:], -scaled[..., :half_width]], axis=-1)
    return grads * cosine[:, None, :] + moved_part


def spread(rows_in):
    return lax.all_gather(rows_in, "tensor", axis=0, tiled=True)


def row_total(term_fn, row_count):
    return lax.psum_scatter(
        term_fn(jnp.int32(0), row_count * lax.axis_size("tensor")),
        "tensor",
        scatter_dimension=0,
        tiled=True,
    )


def pair_total(first_sum, second_sum):
    return lax.psum((first_sum, second_sum), "tensor")


def rows_of(source, first_row, row_count):
    return lax.dynamic_slice_in_dim(source, first_row, row_count, 0)


def head_scores(query_rot, key_rot, allowed):
    scores = jnp.einsum(
        "qhd,khd->hqk", query_rot, key_rot, preferred_element_type=jnp.float32
    ) * HD ** (-0.5)
    return jnp.where(allowed[None], scores, NEG_FILL)


def norm_back(source, inv_scale, gain_vec, grad_in):
    scaled = grad_in * gain_vec
    return inv_scale * scaled - source * inv_scale**3 * jnp.mean(
        source * scaled, axis=1, keepdims=True
    )


def forward(inputs_rows, position_ids, block_row, weights, gain_shards):
    query_w, key_w, value_w, out_w, gate_w, up_w, down_w = weights
    query_g, key_g, attn_g, ffn_g = gain_shards
    local_rows = inputs_rows.shape[0]
    tok_full = spread(inputs_rows)
    seq_len = tok_full.shape[0]
    head_count = query_w.shape[1] // HD
    query_pre = jnp.dot(tok_full, query_w, preferred_element_type=jnp.float32)
    key_pre = jnp.dot(tok_full, key_w, preferred_element_type=jnp.float32)
    value_low = jnp.dot(tok_full, value_w, preferred_element_type=jnp.float32).astype(jnp.bfloat16)
    query_sq, key_sq = pair_total(
        jnp.sum(query_pre * query_pre, axis=1), jnp.sum(key_pre * key_pre, axis=1)
    )
    query_inv = lax.rsqrt(query_sq / D + EPS)[:, None]
    key_inv = lax.rsqrt(key_sq / D + EPS)[:, None]
    cosine, sine = rope_tables(position_ids)
    allowed = block_row[None, :] <= block_row[:, None]
    query_rot = turn_heads(
        (query_pre * query_inv * query_g).reshape(seq_len, head_count, HD), cosine, sine
    ).astype(jnp.bfloat16)
    key_rot = turn_heads(
        (key_pre * key_inv * key_g).reshape(seq_len, head_count, HD), cosine, sine
    ).astype(jnp.bfloat16)
    scores = head_scores(query_rot, key_rot, allowed)
    row_max = jnp.max(scores, axis=2, keepdims=True)
    exp_scores = jnp.exp(scores - row_max)
    exp_total = jnp.sum(exp_scores, axis=2, keepdims=True)
    probs_low = (exp_scores / exp_total).astype(jnp.bfloat16)
    log_total = row_max + jnp.log(exp_total)
    value_heads = value_low.reshape(seq_len, head_count, HD)
    attended = jnp.einsum(
        "hqk,khd->qhd", probs_low, value_heads, preferred_element_type=jnp.float32
    )
    attended = attended.reshape(seq_len, head_count * HD).astype(jnp.bfloat16)

    def attn_term(first_row, row_count):
        return jnp.einsum(
            "rc,oc->ro",
            rows_of(attended, first_row, row_count),
            out_w,
            preferred_element_type=jnp.float32,
        )

    attn_rows = row_total(attn_term, local_rows)
    attn_inv = lax.rsqrt(jnp.mean(attn_rows * attn_rows, axis=1, keepdims=True) + EPS)
    hidden_rows = inputs_rows.astype(jnp.float32) + attn_rows * attn_inv * attn_g
    mid_full = spread(hidden_rows.astype(jnp.bfloat16))
    gate_pre = jnp.dot(mid_full, gate_w, preferred_element_type=jnp.float32)
    up_pre = jnp.dot(mid_full, up_w, preferred_element_type=jnp.float32)
    mixed = (jax.nn.silu(gate_pre) * up_pre).astype(jnp.bfloat16)

    def ffn_term(first_row, row_count):
        return jnp.einsum(
            "rc,oc->ro",
            rows_of(mixed, first_row, row_count),
            down_w,
            preferred_element_type=jnp.float32,
        )

    ffn_rows = row_total(ffn_term, local_rows)
    ffn_inv = lax.rsqrt(jnp.mean(ffn_rows * ffn_rows, axis=1, keepdims=True) + EPS)
    output_rows = hidden_rows + ffn_rows * ffn_inv * ffn_g
    kept_state = dict(
        tok_full=tok_full,
        query_pre=query_pre,
        key_pre=key_pre,
        value_heads=value_heads,
        query_inv=query_inv,
        key_inv=key_inv,
        cosine=cosine,
        sine=sine,
        allowed=allowed,
        query_rot=query_rot,
        key_rot=key_rot,
        log_total=log_total,
        attended=attended,
        attn_rows=attn_rows,
        attn_inv=attn_inv,
        mid_full=mid_full,
        gate_pre=gate_pre,
        up_pre=up_pre,
        mixed=mixed,
        ffn_rows=ffn_rows,
        ffn_inv=ffn_inv,
    )
    return (output_rows.astype(jnp.bfloat16), kept_state)


def backward(cot_rows, kept_state, weights, gain_shards):
    query_w, key_w, value_w, out_w, gate_w, up_w, down_w = weights
    query_g, key_g, attn_g, ffn_g = gain_shards
    local_rows = cot_rows.shape[0]
    tok_full = kept_state["tok_full"]
    query_pre = kept_state["query_pre"]
    key_pre = kept_state["key_pre"]
    query_inv = kept_state["query_inv"]
    key_inv = kept_state["key_inv"]
    cosine = kept_state["cosine"]
    sine = kept_state["sine"]
    query_rot = kept_state["query_rot"]
    key_rot = kept_state["key_rot"]
    attended = kept_state["attended"]
    attn_rows = kept_state["attn_rows"]
    attn_inv = kept_state["attn_inv"]
    mid_full = kept_state["mid_full"]
    gate_pre = kept_state["gate_pre"]
    up_pre = kept_state["up_pre"]
    ffn_rows = kept_state["ffn_rows"]
    ffn_inv = kept_state["ffn_inv"]
    seq_len, head_count = (query_rot.shape[0], query_rot.shape[1])
    ffn_back = norm_back(ffn_rows, ffn_inv, ffn_g, cot_rows)
    ffn_gain_part = jnp.sum(cot_rows * ffn_rows * ffn_inv, axis=0)
    ffn_back_full = spread(ffn_back.astype(jnp.bfloat16))
    mixed_grad = jnp.dot(ffn_back_full, down_w, preferred_element_type=jnp.float32)
    down_wgrad = jnp.einsum(
        "ro,rc->oc", ffn_back_full, kept_state["mixed"], preferred_element_type=jnp.float32
    )
    gate_sig = jax.nn.sigmoid(gate_pre)
    gate_low = (mixed_grad * up_pre * gate_sig * (1.0 + gate_pre * (1.0 - gate_sig))).astype(
        jnp.bfloat16
    )
    up_low = (mixed_grad * gate_pre * gate_sig).astype(jnp.bfloat16)
    gate_wgrad = jnp.einsum("rd,rc->dc", mid_full, gate_low, preferred_element_type=jnp.float32)
    up_wgrad = jnp.einsum("rd,rc->dc", mid_full, up_low, preferred_element_type=jnp.float32)

    def mid_term(first_row, row_count):
        gate_part = jnp.einsum(
            "rc,dc->rd",
            rows_of(gate_low, first_row, row_count),
            gate_w,
            preferred_element_type=jnp.float32,
        )
        up_part = jnp.einsum(
            "rc,dc->rd",
            rows_of(up_low, first_row, row_count),
            up_w,
            preferred_element_type=jnp.float32,
        )
        return gate_part + up_part

    hidden_grad = cot_rows + row_total(mid_term, local_rows)
    attn_back = norm_back(attn_rows, attn_inv, attn_g, hidden_grad)
    attn_gain_part = jnp.sum(hidden_grad * attn_rows * attn_inv, axis=0)
    attn_back_full = spread(attn_back.astype(jnp.bfloat16))
    attended_grad = jnp.dot(attn_back_full, out_w, preferred_element_type=jnp.float32).astype(
        jnp.bfloat16
    )
    out_wgrad = jnp.einsum(
        "ro,rc->oc", attn_back_full, attended, preferred_element_type=jnp.float32
    )
    attended_grad = attended_grad.reshape(seq_len, head_count, HD)
    scores = head_scores(query_rot, key_rot, kept_state["allowed"])
    probs = jnp.exp(scores - kept_state["log_total"])
    prob_grad = jnp.einsum(
        "qhd,khd->hqk", attended_grad, kept_state["value_heads"], preferred_element_type=jnp.float32
    )
    inner_sum = jnp.sum(probs * prob_grad, axis=2, keepdims=True)
    score_low = (probs * (prob_grad - inner_sum)).astype(jnp.bfloat16)
    query_rot_grad = jnp.einsum(
        "hqk,khd->qhd", score_low, key_rot, preferred_element_type=jnp.float32
    ) * HD ** (-0.5)
    key_rot_grad = jnp.einsum(
        "hqk,qhd->khd", score_low, query_rot, preferred_element_type=jnp.float32
    ) * HD ** (-0.5)
    value_low = jnp.einsum(
        "hqk,qhd->khd",
        probs.astype(jnp.bfloat16),
        attended_grad,
        preferred_element_type=jnp.float32,
    )
    value_low = value_low.reshape(seq_len, head_count * HD).astype(jnp.bfloat16)
    query_norm_grad = turn_back(query_rot_grad, cosine, sine).reshape(seq_len, head_count * HD)
    key_norm_grad = turn_back(key_rot_grad, cosine, sine).reshape(seq_len, head_count * HD)
    query_gain_part = jnp.sum(query_norm_grad * query_pre * query_inv, axis=0)
    key_gain_part = jnp.sum(key_norm_grad * key_pre * key_inv, axis=0)
    query_scaled = query_norm_grad * query_g
    key_scaled = key_norm_grad * key_g
    query_dot, key_dot = pair_total(
        jnp.sum(query_pre * query_scaled, axis=1), jnp.sum(key_pre * key_scaled, axis=1)
    )
    query_low = (
        query_inv * query_scaled - query_pre * query_inv**3 * (query_dot / D)[:, None]
    ).astype(jnp.bfloat16)
    key_low = (key_inv * key_scaled - key_pre * key_inv**3 * (key_dot / D)[:, None]).astype(
        jnp.bfloat16
    )
    query_wgrad = jnp.einsum("rd,rc->dc", tok_full, query_low, preferred_element_type=jnp.float32)
    key_wgrad = jnp.einsum("rd,rc->dc", tok_full, key_low, preferred_element_type=jnp.float32)
    value_wgrad = jnp.einsum("rd,rc->dc", tok_full, value_low, preferred_element_type=jnp.float32)

    def input_term(first_row, row_count):
        total_term = jnp.einsum(
            "rc,dc->rd",
            rows_of(query_low, first_row, row_count),
            query_w,
            preferred_element_type=jnp.float32,
        )
        total_term = total_term + jnp.einsum(
            "rc,dc->rd",
            rows_of(key_low, first_row, row_count),
            key_w,
            preferred_element_type=jnp.float32,
        )
        return total_term + jnp.einsum(
            "rc,dc->rd",
            rows_of(value_low, first_row, row_count),
            value_w,
            preferred_element_type=jnp.float32,
        )

    input_rows = hidden_grad + row_total(input_term, local_rows)
    weight_grads = (
        query_wgrad,
        key_wgrad,
        value_wgrad,
        out_wgrad,
        gate_wgrad,
        up_wgrad,
        down_wgrad,
    )
    gain_parts = (query_gain_part, key_gain_part, attn_gain_part, ffn_gain_part)
    return (input_rows, weight_grads, gain_parts)


def body(
    inputs,
    query_weight,
    key_weight,
    value_weight,
    out_weight,
    query_gain,
    key_gain,
    attn_gain,
    gate_weight,
    up_weight,
    down_weight,
    ffn_gain,
    positions,
    block_ids,
    cotangent,
):
    shards = (
        query_weight,
        key_weight,
        value_weight,
        out_weight,
        gate_weight,
        up_weight,
        down_weight,
    )
    gain_shards = (query_gain, key_gain, attn_gain, ffn_gain)
    outputs = []
    input_grads = []
    grad_sums = None
    gain_sums = None
    for micro_idx in range(inputs.shape[0]):
        weights = (
            lax.all_gather(shards[0], "dp", axis=0, tiled=True),
            lax.all_gather(shards[1], "dp", axis=0, tiled=True),
            lax.all_gather(shards[2], "dp", axis=0, tiled=True),
            lax.all_gather(shards[3], "dp", axis=0, tiled=True),
            lax.all_gather(shards[4], "dp", axis=0, tiled=True),
            lax.all_gather(shards[5], "dp", axis=0, tiled=True),
            lax.all_gather(shards[6], "dp", axis=0, tiled=True),
        )
        output_rows, kept_state = forward(
            inputs[micro_idx], positions[micro_idx], block_ids[micro_idx], weights, gain_shards
        )
        input_rows, weight_grads, gain_parts = backward(
            cotangent[micro_idx], kept_state, weights, gain_shards
        )
        grad_sums = (
            weight_grads if grad_sums is None else jax.tree.map(jnp.add, grad_sums, weight_grads)
        )
        gain_sums = (
            gain_parts if gain_sums is None else jax.tree.map(jnp.add, gain_sums, gain_parts)
        )
        outputs.append(output_rows)
        input_grads.append(input_rows)
    grad_sums = (
        lax.psum_scatter(
            grad_sums[0].astype(jnp.bfloat16), "dp", scatter_dimension=0, tiled=True
        ).astype(jnp.float32),
        lax.psum_scatter(
            grad_sums[1].astype(jnp.bfloat16), "dp", scatter_dimension=0, tiled=True
        ).astype(jnp.float32),
        lax.psum_scatter(
            grad_sums[2].astype(jnp.bfloat16), "dp", scatter_dimension=0, tiled=True
        ).astype(jnp.float32),
        lax.psum_scatter(
            grad_sums[3].astype(jnp.bfloat16), "dp", scatter_dimension=0, tiled=True
        ).astype(jnp.float32),
        lax.psum_scatter(
            grad_sums[4].astype(jnp.bfloat16), "dp", scatter_dimension=0, tiled=True
        ).astype(jnp.float32),
        lax.psum_scatter(
            grad_sums[5].astype(jnp.bfloat16), "dp", scatter_dimension=0, tiled=True
        ).astype(jnp.float32),
        lax.psum_scatter(
            grad_sums[6].astype(jnp.bfloat16), "dp", scatter_dimension=0, tiled=True
        ).astype(jnp.float32),
    )
    part_width = query_gain.shape[0]
    offset = lax.axis_index("tensor") * part_width
    query_full = lax.dynamic_update_slice(jnp.zeros((D,), jnp.float32), gain_sums[0], (offset,))
    key_full = lax.dynamic_update_slice(jnp.zeros((D,), jnp.float32), gain_sums[1], (offset,))
    query_total, key_total, attn_total, ffn_total = lax.psum(
        (query_full, key_full, gain_sums[2], gain_sums[3]), ("dp", "tensor")
    )
    query_gain_grad = lax.dynamic_slice(query_total, (offset,), (part_width,))
    key_gain_grad = lax.dynamic_slice(key_total, (offset,), (part_width,))
    return (
        jnp.stack(outputs, axis=0),
        jnp.stack(input_grads, axis=0),
        grad_sums[0],
        grad_sums[1],
        grad_sums[2],
        grad_sums[3],
        query_gain_grad,
        key_gain_grad,
        attn_total,
        grad_sums[4],
        grad_sums[5],
        grad_sums[6],
        ffn_total,
    )


def solution(mesh):
    return jax.shard_map(
        body,
        mesh=mesh,
        in_specs=(
            P("dp", "tensor", None),
            P("dp", "tensor"),
            P("dp", "tensor"),
            P("dp", "tensor"),
            P("dp", "tensor"),
            P("tensor"),
            P("tensor"),
            P(),
            P("dp", "tensor"),
            P("dp", "tensor"),
            P("dp", "tensor"),
            P(),
            P("dp", None),
            P("dp", None),
            P("dp", "tensor", None),
        ),
        out_specs=(
            P("dp", "tensor", None),
            P("dp", "tensor", None),
            P("dp", "tensor"),
            P("dp", "tensor"),
            P("dp", "tensor"),
            P("dp", "tensor"),
            P("tensor"),
            P("tensor"),
            P(),
            P("dp", "tensor"),
            P("dp", "tensor"),
            P("dp", "tensor"),
            P(),
        ),
        check_vma=False,
    )
```

profile of v0, /device:TPU:0, one launch (start us, length us, event | category | flops | bytes accessed | tf_op | source)
XLA Modules:
  0.0 1927.2 jit_solution(6670611586076757327)
XLA Ops:
  16.7 18.8 all-gather.46.cloned.1.call-done
  35.5 51.4 %all-gather.20.cloned.1.call-done = bf16[2048,512]{1,0:T(8,128)(2,1)} async-done(((bf16[256,512]{1,0:T(8,128)(2,1)}), bf16[2048,512]{1,0:T(8,128)(2,1)}) %all-gather.20.cloned.1.call-update) | async-done | bytes 2097168 | tf_op jit(solution)/shard_map/all_gather | solution.py:327
  90.5 46.4 %all-gather.22.cloned.1.call-done = bf16[2048,512]{1,0:T(8,128)(2,1)} async-done(((bf16[256,512]{1,0:T(8,128)(2,1)}), bf16[2048,512]{1,0:T(8,128)(2,1)}) %all-gather.22.cloned.1.call-update) | async-done | bytes 2097168 | tf_op jit(solution)/shard_map/all_gather | solution.py:328
  140.7 19.2 all-gather.44.cloned.1.call-done
  183.9 27.4 %all-gather.18.cloned.1.call-done = bf16[2048,512]{1,0:T(8,128)(2,1)} async-done(((bf16[256,512]{1,0:T(8,128)(2,1)}), bf16[2048,512]{1,0:T(8,128)(2,1)}) %all-gather.18.cloned.1.call-update) | async-done | bytes 2097168 | tf_op jit(solution)/shard_map/all_gather | solution.py:329
  216.0 45.1 %all-gather.24.cloned.1.call-done = bf16[2048,512]{1,0:T(8,128)(2,1)} async-done(((bf16[256,512]{1,0:T(8,128)(2,1)}), bf16[2048,512]{1,0:T(8,128)(2,1)}) %all-gather.24.cloned.1.call-update) | async-done | bytes 2097168 | tf_op jit(solution)/shard_map/all_gather | solution.py:330
  279.5 29.8 %reduce-scatter.20.cloned.1.call-done = f32[128,2048]{1,0:T(8,128)} async-done(((f32[512,2048]{1,0:T(8,128)}), f32[128,2048]{1,0:T(8,128)}) %reduce-scatter.20.cloned.1.call-update) | async-done | bytes 1048592 | tf_op jit(solution)/shard_map/reduce_scatter | solution.py:40
  310.6 45.9 %reduce-scatter.16.cloned.1.call-done = f32[128,2048]{1,0:T(8,128)} async-done(((f32[512,2048]{1,0:T(8,128)}), f32[128,2048]{1,0:T(8,128)}) %reduce-scatter.16.cloned.1.call-update) | async-done | bytes 1048592 | tf_op jit(solution)/shard_map/reduce_scatter | solution.py:40
  363.2 120.4 %all-gather.28.cloned.1.call-done = bf16[2048,2048]{1,0:T(8,128)(2,1)} async-done(((bf16[256,2048]{1,0:T(8,128)(2,1)}), bf16[2048,2048]{1,0:T(8,128)(2,1)}) %all-gather.28.cloned.1.call-update) | async-done | bytes 8388624 | tf_op jit(solution)/shard_map/all_gather | solution.py:331
  483.6 22.8 %all-gather.26.cloned.1.call-done = bf16[512,2048]{1,0:T(8,128)(2,1)} async-done(((bf16[128,2048]{1,0:T(8,128)(2,1)}), bf16[512,2048]{1,0:T(8,128)(2,1)}) %all-gather.26.cloned.1.call-update) | async-done | bytes 2097168 | tf_op jit(solution)/shard_map/all_gather | solution.py:36
  517.0 116.5 %all-gather.30.cloned.1.call-done = bf16[2048,2048]{1,0:T(8,128)(2,1)} async-done(((bf16[256,2048]{1,0:T(8,128)(2,1)}), bf16[2048,2048]{1,0:T(8,128)(2,1)}) %all-gather.30.cloned.1.call-update) | async-done | bytes 8388624 | tf_op jit(solution)/shard_map/all_gather | solution.py:332
  644.2 114.3 %all-gather.32.cloned.1.call-done = bf16[2048,2048]{1,0:T(8,128)(2,1)} async-done(((bf16[256,2048]{1,0:T(8,128)(2,1)}), bf16[2048,2048]{1,0:T(8,128)(2,1)}) %all-gather.32.cloned.1.call-update) | async-done | bytes 8388624 | tf_op jit(solution)/shard_map/all_gather | solution.py:333
  769.6 11.9 all-gather.34.cloned.1.call-done
  790.1 12.5 multiply_convert_fusion.6
  810.2 18.2 reduce-scatter.18.cloned.1.call-done
  829.9 45.6 %reduce-scatter.22.cloned.1.call-done = f32[128,2048]{1,0:T(8,128)} async-done(((f32[512,2048]{1,0:T(8,128)}), f32[128,2048]{1,0:T(8,128)}) %reduce-scatter.22.cloned.1.call-update) | async-done | bytes 1048592 | tf_op jit(solution)/shard_map/reduce_scatter | solution.py:40
  882.0 21.9 %all-gather.40.cloned.1.call-done = bf16[512,2048]{1,0:T(8,128)(2,1)} async-done(((bf16[128,2048]{1,0:T(8,128)(2,1)}), bf16[512,2048]{1,0:T(8,128)(2,1)}) %all-gather.40.cloned.1.call-update) | async-done | bytes 2097168 | tf_op jit(solution)/shard_map/all_gather | solution.py:36
  903.9 12.1 multiply_convert_fusion.1
  934.4 12.6 multiply_convert_fusion.4
  965.1 13.7 reduce-scatter.28.cloned.1.call-done
  978.8 47.2 %reduce-scatter.24.cloned.1.call-done = f32[128,2048]{1,0:T(8,128)} async-done(((f32[512,2048]{1,0:T(8,128)}), f32[128,2048]{1,0:T(8,128)}) %reduce-scatter.24.cloned.1.call-update) | async-done | bytes 1048592 | tf_op jit(solution)/shard_map/reduce_scatter | solution.py:40
  1034.4 21.9 %all-gather.38.cloned.1.call-done = bf16[512,2048]{1,0:T(8,128)(2,1)} async-done(((bf16[128,2048]{1,0:T(8,128)(2,1)}), bf16[512,2048]{1,0:T(8,128)(2,1)}) %all-gather.38.cloned.1.call-update) | async-done | bytes 2097168 | tf_op jit(solution)/shard_map/all_gather | solution.py:36
  1061.2 19.8 %all-gather.42.cloned.1.call-done = bf16[512,2048]{1,0:T(8,128)(2,1)} async-done(((bf16[128,2048]{1,0:T(8,128)(2,1)}), bf16[512,2048]{1,0:T(8,128)(2,1)}) %all-gather.42.cloned.1.call-update) | async-done | bytes 2097168 | tf_op jit(solution)/shard_map/all_gather | solution.py:36
  1136.9 12.8 fusion.101
  1223.3 41.7 %all-reduce = (f32[2048]{0:T(1024)S(1)}, f32[2048]{0:T(1024)S(1)}, f32[2048]{0:T(1024)}, f32[2048]{0:T(1024)}) all-reduce(f32[2048]{0:T(1024)S(1)} %add_dynamic-update-slice_fusion.1, f32[2048]{0:T(1024)S(1)} %add_dynamic-update-slice_fusion, f32[2048]{0:T(1024)S(1)} %add.292, ...), channel_id=1, replica_groups=mesh['dp'=8,'tensor'=4] {'dp','tensor'}, use_global_device_ids=true, to_apply=%region_44.45 | all-reduce | flops 8192 | bytes 65536 | tf_op jit(solution)/shard_map/psum | solution.py:376
  1270.0 27.4 %reduce-scatter.32.cloned.1.call-done = bf16[256,512]{0,1:T(8,128)(2,1)} async-done(((bf16[2048,512]{0,1:T(8,128)(2,1)}), bf16[256,512]{0,1:T(8,128)(2,1)}) %reduce-scatter.32.cloned.1.call-update) | async-done | bytes 262160 | tf_op jit(solution)/shard_map/reduce_scatter | solution.py:350
  1299.3 69.3 %reduce-scatter.36.cloned.1.call-done = bf16[256,512]{0,1:T(8,128)(2,1)} async-done(((bf16[2048,512]{0,1:T(8,128)(2,1)}), bf16[256,512]{0,1:T(8,128)(2,1)}) %reduce-scatter.36.cloned.1.call-update) | async-done | bytes 262160 | tf_op jit(solution)/shard_map/reduce_scatter | solution.py:356
  1370.5 149.7 %reduce-scatter.44.cloned.1.call-done = bf16[256,2048]{1,0:T(8,128)(2,1)} async-done(((bf16[2048,2048]{1,0:T(8,128)(2,1)}), bf16[256,2048]{1,0:T(8,128)(2,1)}) %reduce-scatter.44.cloned.1.call-update) | async-done | bytes 1048592 | tf_op jit(solution)/shard_map/reduce_scatter | solution.py:368
  1523.0 149.2 %reduce-scatter.42.cloned.1.call-done = bf16[256,2048]{1,0:T(8,128)(2,1)} async-done(((bf16[2048,2048]{1,0:T(8,128)(2,1)}), bf16[256,2048]{1,0:T(8,128)(2,1)}) %reduce-scatter.42.cloned.1.call-update) | async-done | bytes 1048592 | tf_op jit(solution)/shard_map/reduce_scatter | solution.py:365
  1675.0 148.9 %reduce-scatter.40.cloned.1.call-done = bf16[256,2048]{1,0:T(8,128)(2,1)} async-done(((bf16[2048,2048]{1,0:T(8,128)(2,1)}), bf16[256,2048]{1,0:T(8,128)(2,1)}) %reduce-scatter.40.cloned.1.call-update) | async-done | bytes 1048592 | tf_op jit(solution)/shard_map/reduce_scatter | solution.py:362
  1826.6 43.5 %reduce-scatter.30.cloned.1.call-done = f32[128,2048]{1,0:T(8,128)} async-done(((f32[512,2048]{1,0:T(8,128)}), f32[128,2048]{1,0:T(8,128)}) %reduce-scatter.30.cloned.1.call-update) | async-done | bytes 1048592 | tf_op jit(solution)/shard_map/reduce_scatter | solution.py:40
  1871.5 45.6 %reduce-scatter.26.cloned.1.call-done = f32[128,2048]{1,0:T(8,128)} async-done(((f32[512,2048]{1,0:T(8,128)}), f32[128,2048]{1,0:T(8,128)}) %reduce-scatter.26.cloned.1.call-update) | async-done | bytes 1048592 | tf_op jit(solution)/shard_map/reduce_scatter | solution.py:40
  (456 shorter events, 327.0 us)
Async XLA Ops:
  7.2 28.3 %all-gather.46.cloned.1.call-start = ((), (), s32[]{:S(2)}) async-start(), calls=%async_computation.44 | async-start | bytes 2621440 | tf_op jit(solution)/shard_map/all_gather | solution.py:36
  9.5 77.4 %all-gather.20.cloned.1.call-start = ((), (), s32[]{:S(2)}) async-start(), calls=%async_computation.16 | async-start | bytes 2359296 | tf_op jit(solution)/shard_map/all_gather | solution.py:327
  10.3 126.6 %all-gather.22.cloned.1.call-start = ((), (), s32[]{:S(2)}) async-start(), calls=%async_computation.17 | async-start | bytes 2359296 | tf_op jit(solution)/shard_map/all_gather | solution.py:328
  11.0 148.9 %all-gather.44.cloned.1.call-start = ((), (), s32[]{:S(2)}) async-start(), calls=%async_computation.43 | async-start | bytes 2621440 | tf_op jit(solution)/shard_map/all_gather | solution.py:36
  11.6 199.7 %all-gather.18.cloned.1.call-start = ((), (), s32[]{:S(2)}) async-start(), calls=%async_computation.15 | async-start | bytes 2359296 | tf_op jit(solution)/shard_map/all_gather | solution.py:329
  12.2 248.9 %all-gather.24.cloned.1.call-start = ((), (), s32[]{:S(2)}) async-start(), calls=%async_computation.18 | async-start | bytes 2359296 | tf_op jit(solution)/shard_map/all_gather | solution.py:330
  12.8 296.4 %reduce-scatter.20.cloned.1.call-start = ((), (), s32[]{:S(2)}) async-start(), calls=%async_computation.25 | async-start | bytes 5242880 | tf_op jit(solution)/shard_map/reduce_scatter | solution.py:40
  266.1 90.4 %reduce-scatter.16.cloned.1.call-start = ((), (), s32[]{:S(2)}) async-start(), calls=%async_computation.19 | async-start | bytes 5242880 | tf_op jit(solution)/shard_map/reduce_scatter | solution.py:40
  278.7 204.9 %all-gather.28.cloned.1.call-start = ((), (), s32[]{:S(2)}) async-start(), calls=%async_computation.21 | async-start | bytes 9437184 | tf_op jit(solution)/shard_map/all_gather | solution.py:331
  279.4 226.9 %all-gather.26.cloned.1.call-start = ((), (), s32[]{:S(2)}) async-start(), calls=%async_computation.20 | async-start | bytes 2621440 | tf_op jit(solution)/shard_map/all_gather | solution.py:36
  360.8 272.7 %all-gather.30.cloned.1.call-start = ((), (), s32[]{:S(2)}) async-start(), calls=%async_computation.22 | async-start | bytes 9437184 | tf_op jit(solution)/shard_map/all_gather | solution.py:332
  361.5 397.0 %all-gather.32.cloned.1.call-start = ((), (), s32[]{:S(2)}) async-start(), calls=%async_computation.23 | async-start | bytes 9437184 | tf_op jit(solution)/shard_map/all_gather | solution.py:333
  362.1 419.4 %all-gather.34.cloned.1.call-start = ((), (), s32[]{:S(2)}) async-start(), calls=%async_computation.26 | async-start | bytes 2621440 | tf_op jit(solution)/shard_map/all_gather | solution.py:36
  362.9 465.6 %reduce-scatter.18.cloned.1.call-start = ((), (), s32[]{:S(2)}) async-start(), calls=%async_computation.24 | async-start | bytes 5242880 | tf_op jit(solution)/shard_map/reduce_scatter | solution.py:40
  769.1 106.4 %reduce-scatter.22.cloned.1.call-start = ((), (), s32[]{:S(2)}) async-start(), calls=%async_computation.27 | async-start | bytes 5242880 | tf_op jit(solution)/shard_map/reduce_scatter | solution.py:40
  810.1 93.8 %all-gather.40.cloned.1.call-start = ((), (), s32[]{:S(2)}) async-start(), calls=%async_computation.32 | async-start | bytes 2621440 | tf_op jit(solution)/shard_map/all_gather | solution.py:36
  881.1 53.2 %all-gather.36.cloned.1.call-start = ((), (), s32[]{:S(2)}) async-start(), calls=%async_computation.28 | async-start | bytes 2621440 | tf_op jit(solution)/shard_map/all_gather | solution.py:36
  881.7 97.0 %reduce-scatter.28.cloned.1.call-start = ((), (), s32[]{:S(2)}) async-start(), calls=%async_computation.33 | async-start | bytes 5242880 | tf_op jit(solution)/shard_map/reduce_scatter | solution.py:40
  934.1 91.9 %reduce-scatter.24.cloned.1.call-start = ((), (), s32[]{:S(2)}) async-start(), calls=%async_computation.29 | async-start | bytes 5242880 | tf_op jit(solution)/shard_map/reduce_scatter | solution.py:40
  965.0 91.3 %all-gather.38.cloned.1.call-start = ((), (), s32[]{:S(2)}) async-start(), calls=%async_computation.30 | async-start | bytes 2621440 | tf_op jit(solution)/shard_map/all_gather | solution.py:36
  1033.6 47.5 %all-gather.42.cloned.1.call-start = ((), (), s32[]{:S(2)}) async-start(), calls=%async_computation.34 | async-start | bytes 2621440 | tf_op jit(solution)/shard_map/all_gather | solution.py:36
  1034.3 232.0 %reduce-scatter.38.cloned.1.call-start = ((), (), s32[]{:S(2)}) async-start(), calls=%async_computation.39 | async-start | bytes 2359296 | tf_op jit(solution)/shard_map/reduce_scatter | solution.py:359
  1086.6 181.5 %reduce-scatter.34.cloned.1.call-start = ((), (), s32[]{:S(2)}) async-start(), calls=%async_computation.37 | async-start | bytes 2359296 | tf_op jit(solution)/shard_map/reduce_scatter | solution.py:353
  1120.6 176.8 %reduce-scatter.32.cloned.1.call-start = ((), (), s32[]{:S(2)}) async-start(), calls=%async_computation.36 | async-start | bytes 2359296 | tf_op jit(solution)/shard_map/reduce_scatter | solution.py:350
  1127.7 240.9 %reduce-scatter.36.cloned.1.call-start = ((), (), s32[]{:S(2)}) async-start(), calls=%async_computation.38 | async-start | bytes 2359296 | tf_op jit(solution)/shard_map/reduce_scatter | solution.py:356
  1136.6 383.6 %reduce-scatter.44.cloned.1.call-start = ((), (), s32[]{:S(2)}) async-start(), calls=%async_computation.42 | async-start | bytes 9437184 | tf_op jit(solution)/shard_map/reduce_scatter | solution.py:368
  1160.0 512.2 %reduce-scatter.42.cloned.1.call-start = ((), (), s32[]{:S(2)}) async-start(), calls=%async_computation.41 | async-start | bytes 9437184 | tf_op jit(solution)/shard_map/reduce_scatter | solution.py:365
  1182.1 641.8 %reduce-scatter.40.cloned.1.call-start = ((), (), s32[]{:S(2)}) async-start(), calls=%async_computation.40 | async-start | bytes 9437184 | tf_op jit(solution)/shard_map/reduce_scatter | solution.py:362
  1202.9 667.2 %reduce-scatter.30.cloned.1.call-start = ((), (), s32[]{:S(2)}) async-start(), calls=%async_computation.35 | async-start | bytes 5242880 | tf_op jit(solution)/shard_map/reduce_scatter | solution.py:40
  1211.9 705.2 %reduce-scatter.26.cloned.1.call-start = ((), (), s32[]{:S(2)}) async-start(), calls=%async_computation.31 | async-start | bytes 5242880 | tf_op jit(solution)/shard_map/reduce_scatter | solution.py:40
  1370.5 499.6 %copy-start.33 = (f32[128,2048]{1,0:T(8,128)S(1)}, f32[128,2048]{1,0:T(8,128)}, u32[]{:S(2)}) copy-start(f32[128,2048]{1,0:T(8,128)} %copy-done.32) | copy-start | bytes 3145732
  1523.0 394.1 %copy-start.31 = (f32[128,2048]{1,0:T(8,128)S(1)}, f32[128,2048]{1,0:T(8,128)}, u32[]{:S(2)}) copy-start(f32[128,2048]{1,0:T(8,128)} %copy-done.30) | copy-start | bytes 3145732
  (131 other events, 1363.4 us)
Sparse Core Ops, SparseCore 0:
  10.2 25.2 all-gather.45
  37.6 49.2 all-gather.19
  89.1 47.7 all-gather.21
  138.9 21.0 all-gather.43
  162.0 49.2 all-gather.17
  213.3 47.7 all-gather.23
  266.2 42.9 reduce-scatter.19
  311.9 44.5 reduce-scatter.15
  358.6 124.9 all-gather.27
  485.5 20.7 all-gather.25
  508.5 124.9 all-gather.29
  635.4 123.1 all-gather.31
  760.7 20.7 all-gather.33
  783.9 44.4 reduce-scatter.17
  831.0 44.4 reduce-scatter.21
  881.3 22.5 all-gather.39
  905.9 22.5 all-gather.35
  934.2 44.4 reduce-scatter.27
  981.4 44.5 reduce-scatter.23
  1033.7 22.5 all-gather.37
  1058.4 22.5 all-gather.41
  1086.7 67.6 reduce-scatter.37
  1158.5 67.3 reduce-scatter.33
  1229.9 67.4 reduce-scatter.31
  1301.5 67.0 reduce-scatter.35
  1372.1 148.0 reduce-scatter.43
  1524.1 148.0 reduce-scatter.41
  1675.8 147.9 reduce-scatter.39
  1826.5 43.5 reduce-scatter.29
  1872.5 44.4 reduce-scatter.25
where the time goes:
time: 1930 us
  waiting for transfers between devices  1500 us (78%)
  matrix products  265 us (14%)
  other arithmetic  59 us (3%)
  blocking collectives  54.6 us (3%)
  local copies, waits for them, and re-layouts  29.2 us (2%)
    reduce_scatter x8, waiting for transfers between devices, row_total(): lax.psum_scatter(term_fn(jnp.int32(0), row_count * lax.axis_size('tensor'...  289 us
    reduce_scatter x1, waiting for transfers between devices, body(): lax.psum_scatter(grad_sums[6].astype(jnp.bfloat16), 'dp', scatter_dimensi...  150 us
    reduce_scatter x1, waiting for transfers between devices, body(): lax.psum_scatter(grad_sums[5].astype(jnp.bfloat16), 'dp', scatter_dimensi...  149 us
    reduce_scatter x1, waiting for transfers between devices, body(): lax.psum_scatter(grad_sums[4].astype(jnp.bfloat16), 'dp', scatter_dimensi...  149 us
    all_gather x8, waiting for transfers between devices, spread(): return lax.all_gather(rows_in, 'tensor', axis=0, tiled=True)  136 us
    all_gather x1, waiting for transfers between devices, body(): lax.all_gather(shards[4], 'dp', axis=0, tiled=True)  120 us
    all_gather x1, waiting for transfers between devices, body(): lax.all_gather(shards[5], 'dp', axis=0, tiled=True)  116 us
    all_gather x1, waiting for transfers between devices, body(): lax.all_gather(shards[6], 'dp', axis=0, tiled=True)  114 us
  transfers between devices with their start and end apart: 30, of which 27 were waited for; matrix products, arithmetic and copies ran while one was open for 16% of the time, Pallas kernels for 0%

commit v1 on v0

v1 whole, which is shorter than its diff:
```python
import jax
import jax.numpy as jnp
from jax import lax
from jax.sharding import PartitionSpec as P

D = 2048
HD = 128
EPS = 1e-06
THETA = 500000.0
NEG_FILL = -1e30
BF = jnp.bfloat16
F32 = jnp.float32


def dot(left, right):
    return jnp.dot(left, right, preferred_element_type=F32)


def dot_nt(left, right):
    return lax.dot_general(left, right, (((1,), (1,)), ((), ())), preferred_element_type=F32)


def dot_tn(left, right):
    return lax.dot_general(left, right, (((0,), (0,)), ((), ())), preferred_element_type=F32)


class Link:
    def __init__(self, axis, perm, depth):
        self.axis = axis
        self.perm = perm
        self.depth = depth
        self.done = []

    def send(self, array):
        if len(self.done) >= self.depth:
            array, _ = lax.optimization_barrier((array, self.done[-self.depth]))
        result = lax.ppermute(array, self.axis, self.perm)
        self.done.append(result)
        return result


def rope_tables(position_ids):
    inv_freq = 1.0 / THETA ** (jnp.arange(0, HD, 2, dtype=F32) / HD)
    angles = position_ids.astype(F32)[:, None] * inv_freq[None, :]
    angles = jnp.concatenate([angles, angles], axis=1)
    return (jnp.cos(angles), jnp.sin(angles))


def turn_heads(values, cosine, sine):
    half_width = values.shape[-1] // 2
    rotated = jnp.concatenate([-values[..., half_width:], values[..., :half_width]], axis=-1)
    return values * cosine[:, None, :] + rotated * sine[:, None, :]


def turn_back(grads, cosine, sine):
    half_width = grads.shape[-1] // 2
    scaled = grads * sine[:, None, :]
    moved_part = jnp.concatenate([scaled[..., half_width:], -scaled[..., :half_width]], axis=-1)
    return grads * cosine[:, None, :] + moved_part


def norm_back(source, inv_scale, gain_vec, grad_in):
    scaled = grad_in * gain_vec
    return inv_scale * scaled - source * inv_scale**3 * jnp.mean(
        source * scaled, axis=1, keepdims=True
    )


def body(
    inputs,
    query_weight,
    key_weight,
    value_weight,
    out_weight,
    query_gain,
    key_gain,
    attn_gain,
    gate_weight,
    up_weight,
    down_weight,
    ffn_gain,
    positions,
    block_ids,
    cotangent,
):
    dp = lax.axis_size("dp")
    ring = dp // 2
    width = D // dp
    pair = 2 * width
    seqs, rows, _ = inputs.shape
    local = seqs * rows
    tokens = 4 * local
    length = 4 * rows
    heads = query_weight.shape[1] // HD
    hw = heads * HD
    dp_index = lax.axis_index("dp")
    place, side = dp_index // 2, dp_index % 2
    t_index = lax.axis_index("tensor")
    t_high, t_low = t_index // 2, t_index % 2

    z_perm = [(i, (i - 2) % dp) for i in range(dp)]
    x_perm = [(i, i ^ 1) for i in range(dp)]
    y_perm = [(i, i ^ 2) for i in range(4)]
    c_perm = [(i, i ^ 1) for i in range(4)]

    def swap_sides(array):
        parts = array.reshape(array.shape[:-1] + (ring, 2, width))
        return jnp.where(side == 1, parts[..., ::-1, :], parts).reshape(array.shape)

    def roll(array, by):
        return lax.dynamic_slice_in_dim(
            jnp.concatenate([array, array], axis=-1), by, D, array.ndim - 1
        )

    def to_own(array):
        return swap_sides(roll(array, place * pair))

    def from_own(array):
        return roll(swap_sides(array), (D - place * pair) % D)

    def flip_rows(array, axis):
        parts = array.reshape(array.shape[:axis] + (2, 2) + array.shape[axis + 1 :])
        parts = jnp.where(t_high == 1, jnp.flip(parts, axis), parts)
        parts = jnp.where(t_low == 1, jnp.flip(parts, axis + 1), parts)
        return parts.reshape(array.shape)

    z_link = Link("dp", z_perm, 2)
    x_link = Link("dp", x_perm, 2)
    y_link = Link("tensor", y_perm, 2)

    def core_send(array):
        return lax.ppermute(array, "tensor", c_perm)

    def spread(own):
        other = core_send(own)
        far = y_link.send(own)
        return jnp.concatenate([own, other, far, core_send(far)], axis=0)

    def row_total(term, source):
        blocks = [source[u * local : (u + 1) * local] for u in range(4)]
        away = core_send(term(jnp.concatenate([blocks[1], blocks[3]], axis=0)))
        far = term(blocks[2]) + away[local:]
        back = y_link.send(far.astype(BF))
        return term(blocks[0]) + away[:local] + back.astype(F32)

    def sum_rows(vectors):
        parts = flip_rows(vectors.reshape(-1, 4, local), 1)
        return flip_rows(lax.psum(parts, "tensor"), 1).reshape(vectors.shape)

    def gather_steps(shard, pair_first):
        own, other = [shard] + [None] * (ring - 1), [None] * ring
        z_ops, x_ops = [], []

        def z_own(s):
            own[s] = z_link.send(own[s - 1])

        def z_other(s):
            other[s] = z_link.send(other[s - 1])

        def x_own(s):
            other[s] = x_link.send(own[s])

        return own, other, z_own, z_other, x_own

    qkv_shard = jnp.concatenate([query_weight, key_weight, value_weight], axis=1)
    streams = {}
    for name, shard in (
        ("qkv", qkv_shard),
        ("out", out_weight),
        ("gate", gate_weight),
        ("up", up_weight),
        ("down", down_weight),
    ):
        streams[name] = gather_steps(shard, name == "qkv")

    def run_z(name, s):
        streams[name][2](s)

    def run_zo(name, s):
        streams[name][3](s)

    def run_x(name, s):
        streams[name][4](s)

    x_own_rows = to_own(inputs.reshape(local, D))
    run_x("qkv", 0)
    tok_full = spread(x_own_rows)
    for s in range(1, ring):
        run_z("qkv", s)
        run_zo("qkv", s)
    for name in ("out", "gate", "up", "down"):
        run_x(name, 0)
    for name in ("out", "gate", "up", "down"):
        for s in range(1, ring):
            run_z(name, s)
            run_x(name, s)

    def stacked(name):
        own, other = streams[name][0], streams[name][1]
        blocks = []
        for s in range(ring):
            blocks += [own[s], other[s]]
        return jnp.concatenate(blocks, axis=0)

    attn_g, ffn_g = to_own(attn_gain[None]), to_own(ffn_gain[None])
    cot_rows = to_own(cotangent.reshape(local, D))

    qkv_w = stacked("qkv")
    pre = dot(tok_full, qkv_w)
    query_pre, key_pre = pre[:, :hw], pre[:, hw : 2 * hw]
    value_low = pre[:, 2 * hw :].astype(BF)
    squares = sum_rows(
        jnp.stack([jnp.sum(query_pre * query_pre, axis=1), jnp.sum(key_pre * key_pre, axis=1)])
    )
    inverses = lax.rsqrt(squares / D + EPS)
    query_inv, key_inv = inverses[0][:, None], inverses[1][:, None]
    own_positions = flip_rows(positions.reshape(seqs, 4, rows), 1)
    cosine, sine = rope_tables(own_positions.transpose(1, 0, 2).reshape(tokens))
    own_ids = flip_rows(block_ids.reshape(seqs, 4, rows), 1).reshape(seqs, length)
    allowed = own_ids[:, None, :] <= own_ids[:, :, None]

    def by_head(array):
        return (
            array.reshape(4, seqs, rows, heads, HD)
            .transpose(1, 3, 0, 2, 4)
            .reshape(seqs, heads, length, HD)
        )

    def by_token(array):
        return (
            array.reshape(seqs, heads, 4, rows, HD).transpose(2, 0, 3, 1, 4).reshape(tokens, hw)
        )

    query_rot = by_head(
        turn_heads(
            (query_pre * query_inv * query_gain).reshape(tokens, heads, HD), cosine, sine
        ).astype(BF)
    )
    key_rot = by_head(
        turn_heads(
            (key_pre * key_inv * key_gain).reshape(tokens, heads, HD), cosine, sine
        ).astype(BF)
    )
    value_heads = by_head(value_low)
    scores = (
        jnp.einsum("shqd,shkd->shqk", query_rot, key_rot, preferred_element_type=F32) * HD**-0.5
    )
    scores = jnp.where(allowed[:, None], scores, NEG_FILL)
    row_max = jnp.max(scores, axis=3, keepdims=True)
    exp_scores = jnp.exp(scores - row_max)
    probs = exp_scores / jnp.sum(exp_scores, axis=3, keepdims=True)
    probs_low = probs.astype(BF)
    attended = by_token(
        jnp.einsum("shqk,shkd->shqd", probs_low, value_heads, preferred_element_type=F32).astype(BF)
    )
    out_w = stacked("out")
    attn_rows = row_total(lambda part: dot_nt(part, out_w), attended)
    attn_inv = lax.rsqrt(jnp.mean(attn_rows * attn_rows, axis=1, keepdims=True) + EPS)
    hidden_rows = x_own_rows.astype(F32) + attn_rows * attn_inv * attn_g
    mid_full = spread(hidden_rows.astype(BF))
    gate_w, up_w = stacked("gate"), stacked("up")
    gate_pre = dot(mid_full, gate_w)
    up_pre = dot(mid_full, up_w)
    gate_sig = jax.nn.sigmoid(gate_pre)
    mixed = (gate_pre * gate_sig * up_pre).astype(BF)
    ffn_parts = []
    down_parts = []
    for s in range(ring):
        piece = jnp.concatenate([streams["down"][0][s], streams["down"][1][s]], axis=0)
        down_parts.append(piece)
        ffn_parts.append(row_total(lambda part, piece=piece: dot_nt(part, piece), mixed))
    down_w = jnp.concatenate(down_parts, axis=0)
    ffn_rows = jnp.concatenate(ffn_parts, axis=1)
    ffn_inv = lax.rsqrt(jnp.mean(ffn_rows * ffn_rows, axis=1, keepdims=True) + EPS)
    output_rows = hidden_rows + ffn_rows * ffn_inv * ffn_g

    def reduce_steps(chunk, pair_first):
        state = {}

        def x_first(s):
            state[("x", s)] = x_link.send(chunk(s, 1).astype(BF))

        def z_hop(s, t=0):
            state[("z", s - 1, t)] = z_link.send(total(s, t).astype(BF))

        def total(s, t):
            value = chunk(s, t)
            if pair_first:
                value = value + state[("x", s)].astype(F32)
            if s < ring - 1 and ("z", s, t) in state:
                value = value + state[("z", s, t)].astype(F32)
            return value

        return state, x_first, z_hop, total

    def reduce_stream(chunk, pair_first):
        received = {}

        def total(s, t):
            value = chunk(s, t)
            if pair_first:
                value = value + received[("x", s)].astype(F32)
            if (s, t) in received:
                value = value + received[(s, t)].astype(F32)
            return value

        def x_send(s):
            received[("x", s)] = x_link.send(chunk(s, 1).astype(BF))

        def z_send(s, t=0):
            received[((s + 1) % ring, t)] = z_link.send(total(s, t).astype(BF))

        def finish():
            if pair_first:
                return total(0, 0)
            back = x_link.send(total(0, 1).astype(BF))
            return total(0, 0) + back.astype(F32)

        return x_send, z_send, finish

    order = list(range(1, ring)) + [0]

    def run_reduce(stream, pair_first):
        x_send, z_send, finish = stream
        if pair_first:
            for s in order:
                x_send(s)
            for s in range(1, ring):
                z_send(s)
        else:
            for s in range(1, ring):
                z_send(s, 0)
                z_send(s, 1)
        return finish()

    def columns(full, s, t):
        return lax.slice_in_dim(full, s * pair + t * width, s * pair + (t + 1) * width, axis=1)

    ffn_back = norm_back(ffn_rows, ffn_inv, ffn_g, cot_rows)
    ffn_gain_part = jnp.sum(cot_rows * ffn_rows * ffn_inv, axis=0)
    ffn_back_low = ffn_back.astype(BF)
    back_parts = {}
    for s in order:
        back_parts[s] = spread(lax.slice_in_dim(ffn_back_low, s * pair, (s + 1) * pair, axis=1))
    ffn_back_full = jnp.concatenate([back_parts[s] for s in range(ring)], axis=1)

    down_grad = run_reduce(
        reduce_stream(
            lambda s, t: dot_tn(
                lax.slice_in_dim(back_parts[s], t * width, (t + 1) * width, axis=1), mixed
            ),
            True,
        ),
        True,
    )
    mixed_grad = dot(ffn_back_full, down_w)
    gate_low = (mixed_grad * up_pre * gate_sig * (1.0 + gate_pre * (1.0 - gate_sig))).astype(BF)
    up_low = (mixed_grad * gate_pre * gate_sig).astype(BF)
    gate_grad = run_reduce(
        reduce_stream(lambda s, t: dot_tn(columns(mid_full, s, t), gate_low), True), True
    )
    gate_up = jnp.concatenate([gate_low, up_low], axis=1)

    def mid_term(part):
        return dot_nt(part[:, : gate_low.shape[1]], gate_w) + dot_nt(
            part[:, gate_low.shape[1] :], up_w
        )

    hidden_grad = cot_rows + row_total(mid_term, gate_up)
    attn_back = norm_back(attn_rows, attn_inv, attn_g, hidden_grad)
    attn_gain_part = jnp.sum(hidden_grad * attn_rows * attn_inv, axis=0)
    attn_back_full = spread(attn_back.astype(BF))
    attended_grad = by_head(dot(attn_back_full, out_w).astype(BF))
    prob_grad = jnp.einsum(
        "shqd,shkd->shqk", attended_grad, value_heads, preferred_element_type=F32
    )
    inner_sum = jnp.sum(probs * prob_grad, axis=3, keepdims=True)
    score_low = (probs * (prob_grad - inner_sum)).astype(BF)
    query_rot_grad = by_token(
        jnp.einsum("shqk,shkd->shqd", score_low, key_rot, preferred_element_type=F32) * HD**-0.5
    )
    key_rot_grad = by_token(
        jnp.einsum("shqk,shqd->shkd", score_low, query_rot, preferred_element_type=F32) * HD**-0.5
    )
    value_back = by_token(
        jnp.einsum(
            "shqk,shqd->shkd", probs_low, attended_grad, preferred_element_type=F32
        ).astype(BF)
    )
    query_norm_grad = turn_back(query_rot_grad.reshape(tokens, heads, HD), cosine, sine).reshape(
        tokens, hw
    )
    key_norm_grad = turn_back(key_rot_grad.reshape(tokens, heads, HD), cosine, sine).reshape(
        tokens, hw
    )
    query_gain_part = jnp.sum(query_norm_grad * query_pre * query_inv, axis=0)
    key_gain_part = jnp.sum(key_norm_grad * key_pre * key_inv, axis=0)
    query_scaled = query_norm_grad * query_gain
    key_scaled = key_norm_grad * key_gain
    dots = sum_rows(
        jnp.stack([jnp.sum(query_pre * query_scaled, axis=1), jnp.sum(key_pre * key_scaled, axis=1)])
    )
    query_dot, key_dot = dots[0][:, None], dots[1][:, None]
    query_low = (
        query_inv * query_scaled - query_pre * query_inv**3 * (query_dot / D)
    ).astype(BF)
    key_low = (key_inv * key_scaled - key_pre * key_inv**3 * (key_dot / D)).astype(BF)
    qkv_low = jnp.concatenate([query_low, key_low, value_back], axis=1)
    input_rows = hidden_grad + row_total(lambda part: dot_nt(part, qkv_w), qkv_low)

    up_grad = run_reduce(
        reduce_stream(lambda s, t: dot_tn(columns(mid_full, s, t), up_low), True), True
    )
    qkv_grad = run_reduce(
        reduce_stream(lambda s, t: dot_tn(columns(tok_full, s, t), qkv_low), False), False
    )
    out_grad = run_reduce(
        reduce_stream(lambda s, t: dot_tn(columns(attn_back_full, s, t), attended), True), True
    )

    offset = t_index * hw
    query_full = lax.dynamic_update_slice(jnp.zeros((D,), F32), query_gain_part, (offset,))
    key_full = lax.dynamic_update_slice(jnp.zeros((D,), F32), key_gain_part, (offset,))
    query_total, key_total, attn_total, ffn_total = lax.psum(
        (query_full, key_full, from_own(attn_gain_part[None])[0], from_own(ffn_gain_part[None])[0]),
        ("dp", "tensor"),
    )
    return (
        from_own(output_rows.astype(BF)).reshape(inputs.shape),
        from_own(input_rows).reshape(inputs.shape),
        qkv_grad[:, :hw],
        qkv_grad[:, hw : 2 * hw],
        qkv_grad[:, 2 * hw :],
        out_grad,
        lax.dynamic_slice(query_total, (offset,), (hw,)),
        lax.dynamic_slice(key_total, (offset,), (hw,)),
        attn_total,
        gate_grad,
        up_grad,
        down_grad,
        ffn_total,
    )


def solution(mesh):
    whole = P()
    both = P("dp", "tensor")
    rows = P("dp", "tensor", None)
    lanes = P("tensor")
    return jax.shard_map(
        body,
        mesh=mesh,
        in_specs=(
            rows, both, both, both, both, lanes, lanes, whole, both, both, both, whole,
            P("dp", None), P("dp", None), rows,
        ),
        out_specs=(
            rows, rows, both, both, both, both, lanes, lanes, whole, both, both, both, whole,
        ),
        check_vma=False,
    )
```

time: 1930 us -> 1180 us (0.61)
  waiting for transfers between devices: 1500 us -> 414 us
  starting transfers between devices: 3.69 us -> 140 us
  local copies, waits for them, and re-layouts: 29.2 us -> 150 us
  matrix products: 265 us -> 320 us
  other arithmetic: 59 us -> 82 us
    reduce_scatter x15 -> x0, waiting for transfers between devices: 834 us -> none  [the longest x8 289 us: row_total(): lax.psum_scatter(term_fn(jnp.int32(0), row_count * lax.axis_size('tensor'...]
    all_gather x15 -> x0, waiting for transfers between devices: 658 us -> none  [the longest x8 136 us: spread(): return lax.all_gather(rows_in, 'tensor', axis=0, tiled=True)]
    ppermute x0 -> x105, waiting for transfers between devices: none -> 414 us  [the longest x84 414 us: send(): result = lax.ppermute(array, self.axis, self.perm)]
    ppermute x0 -> x105, starting transfers between devices: none -> 140 us  [the longest x84 137 us: send(): result = lax.ppermute(array, self.axis, self.perm)]
    dot_general x54 -> x74, matrix products: 265 us -> 314 us  [the longest x24 107 us: dot_nt(): lax.dot_general(left, right, (((1,), (1,)), ((), ())), preferred_element_...]
    unnamed x269 -> x354, local copies, waits for them, and re-layouts: 25.6 us -> 64.1 us
    reshape x0 -> x22, local copies, waits for them, and re-layouts: none -> 35.2 us  [the longest x6 10.3 us: swap_sides(): return jnp.where(side == 1, parts[..., ::-1, :], parts).reshape(array.shape)]
    rev x0 -> x13, local copies, waits for them, and re-layouts: none -> 29.9 us  [the longest x7 29.5 us: swap_sides(): return jnp.where(side == 1, parts[..., ::-1, :], parts).reshape(array.shape)]
  transfers between devices with their start and end apart: 30 -> 105, of which waited for: 27 -> 48; matrix products, arithmetic and copies ran while one was open for 16% -> 41% of each run, Pallas kernels for 0% -> 0%
where the time goes in v1:
time: 1180 us; the launch traced here: 1170 us
  waiting for transfers between devices  414 us (35%)
  matrix products  320 us (27%)
  local copies, waits for them, and re-layouts  150 us (13%)
  starting transfers between devices  140 us (12%)
  other arithmetic  82 us (7%)
  blocking collectives  58.5 us (5%)
    ppermute x84, waiting for transfers between devices, send(): result = lax.ppermute(array, self.axis, self.perm)  414 us
    ppermute x84, starting transfers between devices, send(): result = lax.ppermute(array, self.axis, self.perm)  137 us
    dot_general x24, matrix products, dot_nt(): lax.dot_general(left, right, (((1,), (1,)), ((), ())), preferred_element_...  107 us
    dot_general x5, matrix products, dot(): return jnp.dot(left, right, preferred_element_type=F32)  102 us
    dot_general x40, matrix products, dot_tn(): lax.dot_general(left, right, (((0,), (0,)), ((), ())), preferred_element_...  88.4 us
    unnamed x354, local copies, waits for them, and re-layouts  64.1 us
    psum x1, blocking collectives, body(): lax.psum((query_full, key_full, from_own(attn_gain_part[None])[0], from_o...  47 us
    rev x7, local copies, waits for them, and re-layouts, swap_sides(): return jnp.where(side == 1, parts[..., ::-1, :], parts).reshape(array.shape)  29.5 us
  transfers between devices with their start and end apart: 105, of which 48 were waited for; matrix products, arithmetic and copies ran while one was open for 41% of the time, Pallas kernels for 0%

profile of v1, /device:TPU:0, one launch (start us, length us, event | category | flops | bytes accessed | tf_op | source)
XLA Modules:
  0.0 1168.4 jit_solution(6462968751131164211)
XLA Ops:
  39.5 9.8 collective-permute-done.1
  52.2 13.3 %collective-permute-done.5 = bf16[256,1536]{1,0:T(8,128)(2,1)S(1)} collective-permute-done((bf16[256,1536]{1,0:T(8,128)(2,1)}, bf16[256,1536]{1,0:T(8,128)(2,1)S(1)}, u32[]{:S(2)}, u32[]{:S(2)}) %collective-permute-start.5) | collective-permute-done | bytes 786464 | tf_op jit(solution)/shard_map/ppermute | solution.py:37
  75.8 11.9 %collective-permute-done.8 = bf16[256,1536]{1,0:T(8,128)(2,1)S(1)} collective-permute-done((bf16[256,1536]{1,0:T(8,128)(2,1)S(1)}, bf16[256,1536]{1,0:T(8,128)(2,1)S(1)}, u32[]{:S(2)}, u32[]{:S(2)}) %collective-permute-start.8) | collective-permute-done | bytes 786464 | tf_op jit(solution)/shard_map/ppermute | solution.py:37
  92.0 12.6 %collective-permute-done.7 = bf16[256,1536]{1,0:T(8,128)(2,1)S(1)} collective-permute-done((bf16[256,1536]{1,0:T(8,128)(2,1)S(1)}, bf16[256,1536]{1,0:T(8,128)(2,1)S(1)}, u32[]{:S(2)}, u32[]{:S(2)}) %collective-permute-start.7) | collective-permute-done | bytes 786464 | tf_op jit(solution)/shard_map/ppermute | solution.py:37
  125.0 8.7 fusion.236
  205.1 9.0 collective-permute-done.25
  222.4 15.5 %collective-permute-done.27 = bf16[256,2048]{1,0:T(8,128)(2,1)} collective-permute-done((bf16[256,2048]{1,0:T(8,128)(2,1)}, bf16[256,2048]{1,0:T(8,128)(2,1)}, u32[]{:S(2)}, u32[]{:S(2)}) %collective-permute-start.27) | collective-permute-done | bytes 1048608 | tf_op jit(solution)/shard_map/ppermute | solution.py:37
  242.2 10.8 collective-permute-start.29
  270.8 14.4 %collective-permute-done.29 = bf16[256,2048]{1,0:T(8,128)(2,1)} collective-permute-done((bf16[256,2048]{1,0:T(8,128)(2,1)}, bf16[256,2048]{1,0:T(8,128)(2,1)}, u32[]{:S(2)}, u32[]{:S(2)}) %collective-permute-start.29) | collective-permute-done | bytes 1048608 | tf_op jit(solution)/shard_map/ppermute | solution.py:37
  326.7 13.3 %collective-permute-done.32 = bf16[256,2048]{1,0:T(8,128)(2,1)S(1)} collective-permute-done((bf16[256,2048]{1,0:T(8,128)(2,1)}, bf16[256,2048]{1,0:T(8,128)(2,1)S(1)}, u32[]{:S(2)}, u32[]{:S(2)}) %collective-permute-start.32) | collective-permute-done | bytes 1048608 | tf_op jit(solution)/shard_map/ppermute | solution.py:37
  340.2 19.5 %collective-permute-done.34 = bf16[256,2048]{1,0:T(8,128)(2,1)S(1)} collective-permute-done((bf16[256,2048]{1,0:T(8,128)(2,1)S(1)}, bf16[256,2048]{1,0:T(8,128)(2,1)S(1)}, u32[]{:S(2)}, u32[]{:S(2)}) %collective-permute-start.34) | collective-permute-done | bytes 1048608 | tf_op jit(solution)/shard_map/ppermute | solution.py:37
  367.2 14.5 %collective-permute-done.43 = bf16[256,2048]{1,0:T(8,128)(2,1)S(1)} collective-permute-done((bf16[256,2048]{1,0:T(8,128)(2,1)S(1)}, bf16[256,2048]{1,0:T(8,128)(2,1)S(1)}, u32[]{:S(2)}, u32[]{:S(2)}) %collective-permute-start.43) | collective-permute-done | bytes 1048608 | tf_op jit(solution)/shard_map/ppermute | solution.py:37
  381.8 23.7 %collective-permute-done.36 = bf16[256,2048]{1,0:T(8,128)(2,1)S(1)} collective-permute-done((bf16[256,2048]{1,0:T(8,128)(2,1)S(1)}, bf16[256,2048]{1,0:T(8,128)(2,1)S(1)}, u32[]{:S(2)}, u32[]{:S(2)}) %collective-permute-start.36) | collective-permute-done | bytes 1048608 | tf_op jit(solution)/shard_map/ppermute | solution.py:37
  409.4 16.4 %collective-permute-done.47 = bf16[256,2048]{1,0:T(8,128)(2,1)S(1)} collective-permute-done((bf16[256,2048]{1,0:T(8,128)(2,1)S(1)}, bf16[256,2048]{1,0:T(8,128)(2,1)S(1)}, u32[]{:S(2)}, u32[]{:S(2)}) %collective-permute-start.47) | collective-permute-done | bytes 1048608 | tf_op jit(solution)/shard_map/ppermute | solution.py:37
  438.3 13.9 %fusion.226 = f32[1024,2048]{1,0:T(8,128)} fusion(bf16[2048,2048]{1,0:T(8,128)(2,1)S(1)} %bitcast.227, bf16[256,2048]{1,0:T(8,128)(2,1)S(1)} %collective-permute-done.24, bf16[256,2048]{1,0:T(8,128)(2,1)S(1)} %collective-permute-done.23, bf16[256,2048]{1,0:T(8,128)(2,1)S(1)} %collective-permute-done.22, bf16[256,2048]{1,0:T(8,128)(2,1)S(1)} %fusion.115), kind=kOutput, calls=%fused_computation.454 | convolution fusion | flops 8606711808 | bytes 20971520 | tf_op jit(solution)/shard_map/dot_general | solution.py:16
  452.2 17.8 %multiply_convert_fusion.3 = (bf16[1024,2048]{1,0:T(8,128)(2,1)S(1)}, f32[1024,2048]{1,0:T(8,128)}) fusion(f32[1024,2048]{1,0:T(8,128)} %fusion.226, bf16[2048,2048]{1,0:T(8,128)(2,1)} %constant_dynamic-update-slice_fusion.35, bf16[256,2048]{1,0:T(8,128)(2,1)} %copy-done.69, bf16[256,2048]{1,0:T(8,128)(2,1)} %copy-done.67, ...), kind=kOutput, calls=%fused_computation.11 | convolution fusion | flops 8619294720 | bytes 33554432 | tf_op jit(solution)/shard_map/dot_general | solution.py:16
  490.3 8.3 collective-permute-done.38
  567.7 56.2 %multiply_convert_fusion.2 = (bf16[1024,2048]{1,0:T(8,128)(2,1)}, bf16[1024,2048]{1,0:T(8,128)(2,1)}) fusion(f32[1024,2048]{1,0:T(8,128)} %fusion.226, f32[1024,2048]{1,0:T(8,128)} %get-tuple-element.266, bf16[2048,2048]{1,0:T(8,128)(2,1)} %get-tuple-element.217, bf16[256,512]{1,0:T(8,128)(2,1)} %copy-done.106, bf16[256,512]{1,0:T(8,128)(2,1)} %copy-done.101, ...), kind=kOutput, calls=%fused_computation.10 | convolution fusion | flops 8684306432 | bytes 37748736 | tf_op jit(solution)/shard_map/dot_general | solution.py:16
  631.5 10.5 fusion.7
  646.6 10.1 fusion.80
  656.7 11.8 %convolution_add_fusion = f32[512,2048]{1,0:T(8,128)} fusion(f32[512,2048]{1,0:T(8,128)} %fusion.80, bf16[2048,2048]{1,0:T(8,128)(2,1)} %constant_dynamic-update-slice_fusion.27, bf16[512,4096]{1,0:T(8,128)(2,1)} %copy-done.29), kind=kOutput, calls=%fused_computation.62 | convolution fusion | flops 4296015872 | bytes 18874368 | tf_op jit(solution)/shard_map/dot_general | solution.py:20
  686.8 16.3 %collective-permute-done.76 = bf16[256,2048]{1,0:T(8,128)(2,1)S(1)} collective-permute-done((bf16[256,2048]{1,0:T(8,128)(2,1)S(1)}, bf16[256,2048]{1,0:T(8,128)(2,1)S(1)}, u32[]{:S(2)}, u32[]{:S(2)}) %collective-permute-start.76) | collective-permute-done | bytes 1048608 | tf_op jit(solution)/shard_map/ppermute | solution.py:37
  713.5 12.1 %collective-permute-done.71 = bf16[256,2048]{1,0:T(8,128)(2,1)S(1)} collective-permute-done((bf16[256,2048]{1,0:T(8,128)(2,1)S(1)}, bf16[256,2048]{1,0:T(8,128)(2,1)S(1)}, u32[]{:S(2)}, u32[]{:S(2)}) %collective-permute-start.71) | collective-permute-done | bytes 1048608 | tf_op jit(solution)/shard_map/ppermute | solution.py:37
  728.3 19.8 %collective-permute-done.77 = bf16[256,2048]{1,0:T(8,128)(2,1)S(1)} collective-permute-done((bf16[256,2048]{1,0:T(8,128)(2,1)S(1)}, bf16[256,2048]{1,0:T(8,128)(2,1)S(1)}, u32[]{:S(2)}, u32[]{:S(2)}) %collective-permute-start.77) | collective-permute-done | bytes 1048608 | tf_op jit(solution)/shard_map/ppermute | solution.py:37
  753.5 17.0 %collective-permute-done.72 = bf16[256,2048]{1,0:T(8,128)(2,1)S(1)} collective-permute-done((bf16[256,2048]{1,0:T(8,128)(2,1)S(1)}, bf16[256,2048]{1,0:T(8,128)(2,1)S(1)}, u32[]{:S(2)}, u32[]{:S(2)}) %collective-permute-start.72) | collective-permute-done | bytes 1048608 | tf_op jit(solution)/shard_map/ppermute | solution.py:37
  776.5 16.5 %collective-permute-done.78 = bf16[256,2048]{1,0:T(8,128)(2,1)S(1)} collective-permute-done((bf16[256,2048]{1,0:T(8,128)(2,1)S(1)}, bf16[256,2048]{1,0:T(8,128)(2,1)S(1)}, u32[]{:S(2)}, u32[]{:S(2)}) %collective-permute-start.78) | collective-permute-done | bytes 1048608 | tf_op jit(solution)/shard_map/ppermute | solution.py:37
  798.9 16.6 %collective-permute-done.73 = bf16[256,2048]{1,0:T(8,128)(2,1)S(1)} collective-permute-done((bf16[256,2048]{1,0:T(8,128)(2,1)S(1)}, bf16[256,2048]{1,0:T(8,128)(2,1)S(1)}, u32[]{:S(2)}, u32[]{:S(2)}) %collective-permute-start.73) | collective-permute-done | bytes 1048608 | tf_op jit(solution)/shard_map/ppermute | solution.py:37
  848.1 12.3 %collective-permute-done.74 = bf16[256,2048]{1,0:T(8,128)(2,1)S(1)} collective-permute-done((bf16[256,2048]{1,0:T(8,128)(2,1)}, bf16[256,2048]{1,0:T(8,128)(2,1)S(1)}, u32[]{:S(2)}, u32[]{:S(2)}) %collective-permute-start.74) | collective-permute-done | bytes 1048608 | tf_op jit(solution)/shard_map/ppermute | solution.py:37
  893.7 12.1 %collective-permute-done.66 = bf16[256,2048]{1,0:T(8,128)(2,1)} collective-permute-done((bf16[256,2048]{1,0:T(8,128)(2,1)}, bf16[256,2048]{1,0:T(8,128)(2,1)}, u32[]{:S(2)}, u32[]{:S(2)}) %collective-permute-start.66) | collective-permute-done | bytes 1048608 | tf_op jit(solution)/shard_map/ppermute | solution.py:37
  1003.5 10.7 collective-permute-done.88
  1018.9 12.2 %collective-permute-done.94 = bf16[256,1536]{1,0:T(8,128)(2,1)S(1)} collective-permute-done((bf16[256,1536]{1,0:T(8,128)(2,1)S(1)}, bf16[256,1536]{1,0:T(8,128)(2,1)S(1)}, u32[]{:S(2)}, u32[]{:S(2)}) %collective-permute-start.94) | collective-permute-done | bytes 786464 | tf_op jit(solution)/shard_map/ppermute | solution.py:37
  1038.9 47.0 %all-reduce = (f32[2048]{0:T(1024)S(1)}, f32[2048]{0:T(1024)S(1)}, f32[2048]{0:T(1024)}, f32[2048]{0:T(1024)}) all-reduce(f32[2048]{0:T(1024)S(1)} %dynamic_update_slice.6, f32[2048]{0:T(1024)S(1)} %dynamic_update_slice.7, f32[2048]{0:T(1024)S(1)} %bitcast.314, ...), channel_id=1, replica_groups=mesh['dp'=8,'tensor'=4] {'dp','tensor'}, use_global_device_ids=true, to_apply=%region_14.15 | all-reduce | flops 8192 | bytes 65536 | tf_op jit(solution)/shard_map/psum | solution.py:424
  (750 shorter events, 650.2 us)
Async XLA Ops:
  23.6 46.1 %collective-permute-start = (bf16[256,2048]{1,0:T(8,128)(2,1)S(1)}, bf16[256,2048]{1,0:T(8,128)(2,1)}, u32[]{:S(2)}, u32[]{:S(2)}) collective-permute-start(bf16[256,2048]{1,0:T(8,128)(2,1)S(1)} %reshape.384), channel_id=1, source_target_pairs={{0,1},{1,0},{2,3},{3,2},{4,5},{5,4},{6,7},{7,6},{8,9},{9,8},{10,11... | collective-permute-start | bytes 3145736 | tf_op jit(solution)/shard_map/ppermute | solution.py:132
  49.3 59.5 %collective-permute-start.2 = (bf16[256,2048]{1,0:T(8,128)(2,1)}, bf16[256,2048]{1,0:T(8,128)(2,1)S(1)}, u32[]{:S(2)}, u32[]{:S(2)}) collective-permute-start(bf16[256,2048]{1,0:T(8,128)(2,1)} %collective-permute-done.1), channel_id=1, source_target_pairs={{0,1},{1,0},{2,3},{3,2},{4,5},{5,4},{6,7},{7,6},{8,9},{9,8},{10,11... | collective-permute-start | bytes 3145736 | tf_op jit(solution)/shard_map/ppermute | solution.py:132
  51.4 58.5 %collective-permute-start.12 = (bf16[256,2048]{1,0:T(8,128)(2,1)}, bf16[256,2048]{1,0:T(8,128)(2,1)S(1)}, u32[]{:S(2)}, u32[]{:S(2)}) collective-permute-start(bf16[256,2048]{1,0:T(8,128)(2,1)} %param.24), channel_id=1, source_target_pairs={{0,4},{4,0},{8,12},{12,8},{16,20},{20,16},{24,28},{28,24},{1,5},{5... | collective-permute-start | bytes 3145736 | tf_op jit(solution)/shard_map/ppermute | solution.py:37
  74.3 112.6 %collective-permute-start.16 = (bf16[256,2048]{1,0:T(8,128)(2,1)}, bf16[256,2048]{1,0:T(8,128)(2,1)}, u32[]{:S(2)}, u32[]{:S(2)}) collective-permute-start(bf16[256,2048]{1,0:T(8,128)(2,1)} %param.25), channel_id=1, source_target_pairs={{0,4},{4,0},{8,12},{12,8},{16,20},{20,16},{24,28},{28,24},{1,5},{5... | collective-permute-start | bytes 3145736 | tf_op jit(solution)/shard_map/ppermute | solution.py:37
  205.1 113.2 %collective-permute-start.20 = (f32[512,2048]{1,0:T(8,128)}, f32[512,2048]{1,0:T(8,128)}, u32[]{:S(2)}, u32[]{:S(2)}) collective-permute-start(f32[512,2048]{1,0:T(8,128)} %fusion.170), channel_id=1, source_target_pairs={{0,1},{1,0},{2,3},{3,2},{4,5},{5,4},{6,7},{7,6},{8,9},{9,8},{10,11... | collective-permute-start | bytes 12582920 | tf_op jit(solution)/shard_map/ppermute | solution.py:132
  221.8 67.7 %collective-permute-start.26 = (bf16[256,2048]{1,0:T(8,128)(2,1)}, bf16[256,2048]{1,0:T(8,128)(2,1)}, u32[]{:S(2)}, u32[]{:S(2)}) collective-permute-start(bf16[256,2048]{1,0:T(8,128)(2,1)} %collective-permute-done.25), channel_id=1, source_target_pairs={{0,4},{4,0},{8,12},{12,8},{16,20},{20,16},{24,28},{28,24},{1,5},{5... | collective-permute-start | bytes 3145736 | tf_op jit(solution)/shard_map/ppermute | solution.py:37
  242.2 43.1 %collective-permute-start.29 = (bf16[256,2048]{1,0:T(8,128)(2,1)}, bf16[256,2048]{1,0:T(8,128)(2,1)}, u32[]{:S(2)}, u32[]{:S(2)}) collective-permute-start(bf16[256,2048]{1,0:T(8,128)(2,1)} %collective-permute-done.27), channel_id=1, source_target_pairs={{0,24},{4,28},{8,0},{12,4},{16,8},{20,12},{24,16},{28,20},{1,25},{... | collective-permute-start | bytes 3145736 | tf_op jit(solution)/shard_map/ppermute | solution.py:37
  318.0 42.2 %collective-permute-start.35 = (bf16[256,2048]{1,0:T(8,128)(2,1)S(1)}, bf16[256,2048]{1,0:T(8,128)(2,1)S(1)}, u32[]{:S(2)}, u32[]{:S(2)}) collective-permute-start(bf16[256,2048]{1,0:T(8,128)(2,1)S(1)} %collective-permute-done.33), channel_id=1, source_target_pairs={{0,24},{4,28},{8,0},{12,4},{16,8},{20,12},{24,16},{28,20},{1,25},{... | collective-permute-start | bytes 3145736 | tf_op jit(solution)/shard_map/ppermute | solution.py:37
  359.7 47.7 %collective-permute-start.40 = (bf16[256,2048]{1,0:T(8,128)(2,1)S(1)}, bf16[256,2048]{1,0:T(8,128)(2,1)S(1)}, u32[]{:S(2)}, u32[]{:S(2)}) collective-permute-start(bf16[256,2048]{1,0:T(8,128)(2,1)S(1)} %collective-permute-done.39), channel_id=1, source_target_pairs={{0,4},{4,0},{8,12},{12,8},{16,20},{20,16},{24,28},{28,24},{1,5},{5... | collective-permute-start | bytes 3145736 | tf_op jit(solution)/shard_map/ppermute | solution.py:37
  360.5 45.0 %collective-permute-start.36 = (bf16[256,2048]{1,0:T(8,128)(2,1)S(1)}, bf16[256,2048]{1,0:T(8,128)(2,1)S(1)}, u32[]{:S(2)}, u32[]{:S(2)}) collective-permute-start(bf16[256,2048]{1,0:T(8,128)(2,1)S(1)} %collective-permute-done.35), channel_id=1, source_target_pairs={{0,4},{4,0},{8,12},{12,8},{16,20},{20,16},{24,28},{28,24},{1,5},{5... | collective-permute-start | bytes 3145736 | tf_op jit(solution)/shard_map/ppermute | solution.py:37
  425.8 53.8 %collective-permute-start.48 = (bf16[256,2048]{1,0:T(8,128)(2,1)S(1)}, bf16[256,2048]{1,0:T(8,128)(2,1)S(1)}, u32[]{:S(2)}, u32[]{:S(2)}) collective-permute-start(bf16[256,2048]{1,0:T(8,128)(2,1)S(1)} %collective-permute-done.47), channel_id=1, source_target_pairs={{0,4},{4,0},{8,12},{12,8},{16,20},{20,16},{24,28},{28,24},{1,5},{5... | collective-permute-start | bytes 3145736 | tf_op jit(solution)/shard_map/ppermute | solution.py:37
  559.0 118.2 %collective-permute-start.75 = (bf16[256,2048]{1,0:T(8,128)(2,1)}, bf16[256,2048]{1,0:T(8,128)(2,1)}, u32[]{:S(2)}, u32[]{:S(2)}) collective-permute-start(bf16[256,2048]{1,0:T(8,128)(2,1)} %convolution_convert_fusion.3), channel_id=1, source_target_pairs={{0,4},{4,0},{8,12},{12,8},{16,20},{20,16},{24,28},{28,24},{1,5},{5... | collective-permute-start | bytes 3145736 | tf_op jit(solution)/shard_map/ppermute | solution.py:37
  565.6 119.3 %collective-permute-start.70 = (bf16[256,2048]{1,0:T(8,128)(2,1)}, bf16[256,2048]{1,0:T(8,128)(2,1)}, u32[]{:S(2)}, u32[]{:S(2)}) collective-permute-start(bf16[256,2048]{1,0:T(8,128)(2,1)} %convolution_convert_fusion.8), channel_id=1, source_target_pairs={{0,4},{4,0},{8,12},{12,8},{16,20},{20,16},{24,28},{28,24},{1,5},{5... | collective-permute-start | bytes 3145736 | tf_op jit(solution)/shard_map/ppermute | solution.py:37
  683.3 133.6 %collective-permute-start.63 = (f32[512,2048]{1,0:T(8,128)S(1)}, f32[512,2048]{1,0:T(8,128)}, u32[]{:S(2)}, u32[]{:S(2)}) collective-permute-start(f32[512,2048]{1,0:T(8,128)S(1)} %copy-done.138), channel_id=1, source_target_pairs={{0,1},{1,0},{2,3},{3,2},{4,5},{5,4},{6,7},{7,6},{8,9},{9,8},{10,11... | collective-permute-start | bytes 12582920 | tf_op jit(solution)/shard_map/ppermute | solution.py:132
  703.1 44.9 %collective-permute-start.77 = (bf16[256,2048]{1,0:T(8,128)(2,1)S(1)}, bf16[256,2048]{1,0:T(8,128)(2,1)S(1)}, u32[]{:S(2)}, u32[]{:S(2)}) collective-permute-start(bf16[256,2048]{1,0:T(8,128)(2,1)S(1)} %convolution_convert_fusion.5), channel_id=1, source_target_pairs={{0,4},{4,0},{8,12},{12,8},{16,20},{20,16},{24,28},{28,24},{1,5},{5... | collective-permute-start | bytes 3145736 | tf_op jit(solution)/shard_map/ppermute | solution.py:37
  725.6 44.9 %collective-permute-start.72 = (bf16[256,2048]{1,0:T(8,128)(2,1)S(1)}, bf16[256,2048]{1,0:T(8,128)(2,1)S(1)}, u32[]{:S(2)}, u32[]{:S(2)}) collective-permute-start(bf16[256,2048]{1,0:T(8,128)(2,1)S(1)} %convolution_convert_fusion.10), channel_id=1, source_target_pairs={{0,4},{4,0},{8,12},{12,8},{16,20},{20,16},{24,28},{28,24},{1,5},{5... | collective-permute-start | bytes 3145736 | tf_op jit(solution)/shard_map/ppermute | solution.py:37
  748.1 44.9 %collective-permute-start.78 = (bf16[256,2048]{1,0:T(8,128)(2,1)S(1)}, bf16[256,2048]{1,0:T(8,128)(2,1)S(1)}, u32[]{:S(2)}, u32[]{:S(2)}) collective-permute-start(bf16[256,2048]{1,0:T(8,128)(2,1)S(1)} %copy-done.139), channel_id=1, source_target_pairs={{0,4},{4,0},{8,12},{12,8},{16,20},{20,16},{24,28},{28,24},{1,5},{5... | collective-permute-start | bytes 3145736 | tf_op jit(solution)/shard_map/ppermute | solution.py:37
  750.8 43.7 %collective-permute-start.82 = (bf16[256,2048]{1,0:T(8,128)(2,1)S(1)}, bf16[256,2048]{1,0:T(8,128)(2,1)S(1)}, u32[]{:S(2)}, u32[]{:S(2)}) collective-permute-start(bf16[256,2048]{1,0:T(8,128)(2,1)S(1)} %fusion.75), channel_id=1, source_target_pairs={{0,24},{4,28},{8,0},{12,4},{16,8},{20,12},{24,16},{28,20},{1,25},{... | collective-permute-start | bytes 3145736 | tf_op jit(solution)/shard_map/ppermute | solution.py:37
  752.3 45.3 %collective-permute-start.83 = (bf16[256,2048]{1,0:T(8,128)(2,1)S(1)}, bf16[256,2048]{1,0:T(8,128)(2,1)S(1)}, u32[]{:S(2)}, u32[]{:S(2)}) collective-permute-start(bf16[256,2048]{1,0:T(8,128)(2,1)S(1)} %fusion.70), channel_id=1, source_target_pairs={{0,24},{4,28},{8,0},{12,4},{16,8},{20,12},{24,16},{28,20},{1,25},{... | collective-permute-start | bytes 3145736 | tf_op jit(solution)/shard_map/ppermute | solution.py:37
  770.5 44.9 %collective-permute-start.73 = (bf16[256,2048]{1,0:T(8,128)(2,1)S(1)}, bf16[256,2048]{1,0:T(8,128)(2,1)S(1)}, u32[]{:S(2)}, u32[]{:S(2)}) collective-permute-start(bf16[256,2048]{1,0:T(8,128)(2,1)S(1)} %convolution_convert_fusion.11), channel_id=1, source_target_pairs={{0,4},{4,0},{8,12},{12,8},{16,20},{20,16},{24,28},{28,24},{1,5},{5... | collective-permute-start | bytes 3145736 | tf_op jit(solution)/shard_map/ppermute | solution.py:37
  793.0 45.0 %collective-permute-start.79 = (bf16[256,2048]{1,0:T(8,128)(2,1)}, bf16[256,2048]{1,0:T(8,128)(2,1)}, u32[]{:S(2)}, u32[]{:S(2)}) collective-permute-start(bf16[256,2048]{1,0:T(8,128)(2,1)} %convolution_convert_fusion.7), channel_id=1, source_target_pairs={{0,4},{4,0},{8,12},{12,8},{16,20},{20,16},{24,28},{28,24},{1,5},{5... | collective-permute-start | bytes 3145736 | tf_op jit(solution)/shard_map/ppermute | solution.py:37
  797.6 43.9 %collective-permute-start.84 = (bf16[256,2048]{1,0:T(8,128)(2,1)}, bf16[256,2048]{1,0:T(8,128)(2,1)}, u32[]{:S(2)}, u32[]{:S(2)}) collective-permute-start(bf16[256,2048]{1,0:T(8,128)(2,1)} %fusion.72), channel_id=1, source_target_pairs={{0,24},{4,28},{8,0},{12,4},{16,8},{20,12},{24,16},{28,20},{1,25},{... | collective-permute-start | bytes 3145736 | tf_op jit(solution)/shard_map/ppermute | solution.py:37
  815.5 44.9 %collective-permute-start.74 = (bf16[256,2048]{1,0:T(8,128)(2,1)}, bf16[256,2048]{1,0:T(8,128)(2,1)S(1)}, u32[]{:S(2)}, u32[]{:S(2)}) collective-permute-start(bf16[256,2048]{1,0:T(8,128)(2,1)} %convolution_convert_fusion.12), channel_id=1, source_target_pairs={{0,4},{4,0},{8,12},{12,8},{16,20},{20,16},{24,28},{28,24},{1,5},{5... | collective-permute-start | bytes 3145736 | tf_op jit(solution)/shard_map/ppermute | solution.py:37
  841.6 42.6 %collective-permute-start.85 = (bf16[256,2048]{1,0:T(8,128)(2,1)}, bf16[256,2048]{1,0:T(8,128)(2,1)}, u32[]{:S(2)}, u32[]{:S(2)}) collective-permute-start(bf16[256,2048]{1,0:T(8,128)(2,1)} %fusion.74), channel_id=1, source_target_pairs={{0,24},{4,28},{8,0},{12,4},{16,8},{20,12},{24,16},{28,20},{1,25},{... | collective-permute-start | bytes 3145736 | tf_op jit(solution)/shard_map/ppermute | solution.py:37
  845.5 44.1 %collective-permute-start.86 = (bf16[256,2048]{1,0:T(8,128)(2,1)}, bf16[256,2048]{1,0:T(8,128)(2,1)}, u32[]{:S(2)}, u32[]{:S(2)}) collective-permute-start(bf16[256,2048]{1,0:T(8,128)(2,1)} %fusion.69), channel_id=1, source_target_pairs={{0,24},{4,28},{8,0},{12,4},{16,8},{20,12},{24,16},{28,20},{1,25},{... | collective-permute-start | bytes 3145736 | tf_op jit(solution)/shard_map/ppermute | solution.py:37
  846.1 65.5 %collective-permute-start.91 = (bf16[256,2048]{1,0:T(8,128)(2,1)}, bf16[256,2048]{1,0:T(8,128)(2,1)}, u32[]{:S(2)}, u32[]{:S(2)}) collective-permute-start(bf16[256,2048]{1,0:T(8,128)(2,1)} %convolution_convert_fusion.1), channel_id=1, source_target_pairs={{0,4},{4,0},{8,12},{12,8},{16,20},{20,16},{24,28},{28,24},{1,5},{5... | collective-permute-start | bytes 3145736 | tf_op jit(solution)/shard_map/ppermute | solution.py:37
  860.4 175.8 %collective-permute-start.99 = (bf16[256,2048]{1,0:T(8,128)(2,1)}, bf16[256,2048]{1,0:T(8,128)(2,1)}, u32[]{:S(2)}, u32[]{:S(2)}) collective-permute-start(bf16[256,2048]{1,0:T(8,128)(2,1)} %convolution_convert_fusion), channel_id=1, source_target_pairs={{0,4},{4,0},{8,12},{12,8},{16,20},{20,16},{24,28},{28,24},{1,5},{5... | collective-permute-start | bytes 3145736 | tf_op jit(solution)/shard_map/ppermute | solution.py:37
  920.3 56.6 %collective-permute-start.92 = (bf16[256,2048]{1,0:T(8,128)(2,1)}, bf16[256,2048]{1,0:T(8,128)(2,1)}, u32[]{:S(2)}, u32[]{:S(2)}) collective-permute-start(bf16[256,2048]{1,0:T(8,128)(2,1)} %fusion.68), channel_id=1, source_target_pairs={{0,24},{4,28},{8,0},{12,4},{16,8},{20,12},{24,16},{28,20},{1,25},{... | collective-permute-start | bytes 3145736 | tf_op jit(solution)/shard_map/ppermute | solution.py:37
  986.0 130.4 %collective-permute-start.68 = (f32[512,2048]{1,0:T(8,128)}, f32[512,2048]{1,0:T(8,128)}, u32[]{:S(2)}, u32[]{:S(2)}) collective-permute-start(f32[512,2048]{1,0:T(8,128)} %fusion.91), channel_id=1, source_target_pairs={{0,1},{1,0},{2,3},{3,2},{4,5},{5,4},{6,7},{7,6},{8,9},{9,8},{10,11... | collective-permute-start | bytes 12582920 | tf_op jit(solution)/shard_map/ppermute | solution.py:132
  1016.2 74.9 %collective-permute-start.89 = (bf16[256,1536]{1,0:T(8,128)(2,1)}, bf16[256,1536]{1,0:T(8,128)(2,1)}, u32[]{:S(2)}, u32[]{:S(2)}) collective-permute-start(bf16[256,1536]{1,0:T(8,128)(2,1)} %fusion.63), channel_id=1, source_target_pairs={{0,24},{4,28},{8,0},{12,4},{16,8},{20,12},{24,16},{28,20},{1,25},{... | collective-permute-start | bytes 2359304 | tf_op jit(solution)/shard_map/ppermute | solution.py:37
  1033.0 62.9 %collective-permute-start.95 = (bf16[256,1536]{1,0:T(8,128)(2,1)}, bf16[256,1536]{1,0:T(8,128)(2,1)}, u32[]{:S(2)}, u32[]{:S(2)}) collective-permute-start(bf16[256,1536]{1,0:T(8,128)(2,1)} %fusion.65), channel_id=1, source_target_pairs={{0,24},{4,28},{8,0},{12,4},{16,8},{20,12},{24,16},{28,20},{1,25},{... | collective-permute-start | bytes 2359304 | tf_op jit(solution)/shard_map/ppermute | solution.py:37
  1036.2 52.5 %collective-permute-start.100 = (bf16[256,512]{1,0:T(8,128)(2,1)}, bf16[256,512]{1,0:T(8,128)(2,1)}, u32[]{:S(2)}, u32[]{:S(2)}) collective-permute-start(bf16[256,512]{1,0:T(8,128)(2,1)} %convolution_convert_fusion.15), channel_id=1, source_target_pairs={{0,4},{4,0},{8,12},{12,8},{16,20},{20,16},{24,28},{28,24},{1,5},{5... | collective-permute-start | bytes 786440 | tf_op jit(solution)/shard_map/ppermute | solution.py:37
  (224 other events, 4508.7 us)

commit v2 on v1

v2 whole, which is shorter than its diff:
```python
import jax
import jax.numpy as jnp
from jax import lax
from jax.sharding import PartitionSpec as P

D = 2048
HD = 128
EPS = 1e-06
THETA = 500000.0
NEG_FILL = -1e30
BF = jnp.bfloat16
F32 = jnp.float32


def dot(left, right):
    return jnp.dot(left, right, preferred_element_type=F32)


def dot_nt(left, right):
    return lax.dot_general(left, right, (((1,), (1,)), ((), ())), preferred_element_type=F32)


def dot_tn(left, right):
    return lax.dot_general(left, right, (((0,), (0,)), ((), ())), preferred_element_type=F32)


def after(array, others):
    return lax.optimization_barrier((array, others))[0]


def rope_tables(position_ids):
    inv_freq = 1.0 / THETA ** (jnp.arange(0, HD, 2, dtype=F32) / HD)
    angles = position_ids.astype(F32)[:, None] * inv_freq[None, :]
    angles = jnp.concatenate([angles, angles], axis=1)
    return (jnp.cos(angles), jnp.sin(angles))


def turn_heads(values, cosine, sine):
    half_width = values.shape[-1] // 2
    rotated = jnp.concatenate([-values[..., half_width:], values[..., :half_width]], axis=-1)
    return values * cosine[:, None, :] + rotated * sine[:, None, :]


def turn_back(grads, cosine, sine):
    half_width = grads.shape[-1] // 2
    scaled = grads * sine[:, None, :]
    moved_part = jnp.concatenate([scaled[..., half_width:], -scaled[..., :half_width]], axis=-1)
    return grads * cosine[:, None, :] + moved_part


def norm_back(source, inv_scale, gain_vec, grad_in):
    scaled = grad_in * gain_vec
    return inv_scale * scaled - source * inv_scale**3 * jnp.mean(
        source * scaled, axis=1, keepdims=True
    )


def body(
    inputs,
    query_weight,
    key_weight,
    value_weight,
    out_weight,
    query_gain,
    key_gain,
    attn_gain,
    gate_weight,
    up_weight,
    down_weight,
    ffn_gain,
    positions,
    block_ids,
    cotangent,
):
    dp = lax.axis_size("dp")
    seqs, rows, _ = inputs.shape
    local = seqs * rows
    tokens = 8 * local
    length = 4 * rows
    hw = query_weight.shape[1] // 2
    heads = hw // HD
    half = D // 2
    side = lax.axis_index("dp") % 2
    t_index = lax.axis_index("tensor")
    t_high, t_low = t_index // 2, t_index % 2

    x_perm = [(i, i ^ 1) for i in range(dp)]
    y_perm = [(i, i ^ 2) for i in range(4)]
    c_perm = [(i, i ^ 1) for i in range(4)]
    z_groups = [list(range(0, dp, 2)), list(range(1, dp, 2))]

    def x_send(array):
        return lax.ppermute(array, "dp", x_perm)

    def y_send(array):
        return lax.ppermute(array, "tensor", y_perm)

    def core_send(array):
        return lax.ppermute(array, "tensor", c_perm)

    def by_side(mine, other, axis):
        return jnp.concatenate(
            [jnp.where(side == 0, mine, other), jnp.where(side == 0, other, mine)], axis=axis
        )

    def column_half(array, which):
        width = array.shape[-1] // 2
        return lax.dynamic_slice_in_dim(array, which * width, width, array.ndim - 1)

    def pair_rows(*weights):
        mine = jnp.concatenate([column_half(w, side) for w in weights], axis=1)
        theirs = jnp.concatenate([column_half(w, 1 - side) for w in weights], axis=1)
        return mine, x_send(theirs)

    def gather(*weights):
        mine, other = pair_rows(*weights)
        return lax.all_gather(
            by_side(mine, other, 0), "dp", axis=0, tiled=True, axis_index_groups=z_groups
        )

    def reduce_grad(features, grads):
        summed = lax.psum_scatter(
            dot_tn(features, grads).astype(BF),
            "dp",
            scatter_dimension=0,
            tiled=True,
            axis_index_groups=z_groups,
        )
        width = summed.shape[0] // 2
        mine = lax.dynamic_slice_in_dim(summed, side * width, width, 0)
        theirs = lax.dynamic_slice_in_dim(summed, (1 - side) * width, width, 0)
        return mine, x_send(theirs)

    def flip_rows(array, axis):
        parts = array.reshape(array.shape[:axis] + (2, 2) + array.shape[axis + 1 :])
        parts = jnp.where(t_high == 1, jnp.flip(parts, axis), parts)
        parts = jnp.where(t_low == 1, jnp.flip(parts, axis + 1), parts)
        return parts.reshape(array.shape)

    def spread(own):
        first, second = own[:, :half], own[:, half:]
        x_first, y_second = x_send(first), y_send(second)
        first_pair = jnp.concatenate([first, x_first], axis=0)
        second_pair = jnp.concatenate([second, y_second], axis=0)
        y_first, x_second = y_send(first_pair), x_send(second_pair)
        low = jnp.concatenate(
            [first, y_first[:local], x_first, y_first[local:]], axis=0
        )
        high = jnp.concatenate([second_pair, x_second], axis=0)
        even = jnp.concatenate([low, high], axis=1)
        odd = core_send(even)
        blocks = []
        for a in range(2):
            for u in range(2):
                at = (2 * a + u) * local
                blocks += [even[at : at + local], odd[at : at + local]]
        return jnp.concatenate(blocks, axis=0)

    def row_total(term, source):
        blocks = [source[i * local : (i + 1) * local] for i in range(8)]
        away = core_send(term(jnp.concatenate(blocks[1::2], axis=0)).astype(BF))
        kept = term(jnp.concatenate(blocks[0::2], axis=0)) + away.astype(F32)
        low, high = kept[:, :half], kept[:, half:]
        x_low = x_send(low[2 * local :].astype(BF))
        y_high = y_send(
            jnp.concatenate([high[local : 2 * local], high[3 * local :]], axis=0).astype(BF)
        )
        low = low[: 2 * local] + x_low.astype(F32)
        high_own = high[:local] + y_high[:local].astype(F32)
        high_other = high[2 * local : 3 * local] + y_high[local:].astype(F32)
        y_low = y_send(low[local:].astype(BF))
        x_high = x_send(high_other.astype(BF))
        return jnp.concatenate(
            [low[:local] + y_low.astype(F32), high_own + x_high.astype(F32)], axis=1
        )

    def sum_rows(vectors):
        parts = flip_rows(vectors.reshape(-1, 2, 4, local), 2)
        parts = lax.psum(parts, "tensor")
        parts = parts + x_send(parts[:, ::-1])
        return flip_rows(parts, 2).reshape(vectors.shape)

    qkv_w = gather(query_weight, key_weight, value_weight)
    out_w = gather(out_weight)
    gate_w = gather(gate_weight)
    up_w = gather(up_weight)
    down_w = gather(down_weight)
    own_tokens = inputs.reshape(local, D)
    tok_full = spread(own_tokens)
    attn_g, ffn_g = attn_gain[None], ffn_gain[None]
    query_g, key_g = column_half(query_gain, side), column_half(key_gain, side)
    cot_rows = cotangent.reshape(local, D)

    pre = dot(tok_full, qkv_w)
    query_pre, key_pre = pre[:, :hw], pre[:, hw : 2 * hw]
    value_low = pre[:, 2 * hw :].astype(BF)
    squares = sum_rows(
        jnp.stack([jnp.sum(query_pre * query_pre, axis=1), jnp.sum(key_pre * key_pre, axis=1)])
    )
    inverses = lax.rsqrt(squares / D + EPS)
    query_inv, key_inv = inverses[0][:, None], inverses[1][:, None]
    marks = jnp.stack([positions, block_ids])
    marks = jnp.stack([marks, x_send(marks)], axis=1)
    marks = flip_rows(marks.reshape(2, 2, seqs, 4, rows), 3)
    cosine, sine = rope_tables(marks[0].transpose(0, 2, 1, 3).reshape(tokens))
    own_ids = marks[1].reshape(2 * seqs, length)
    allowed = own_ids[:, None, :] <= own_ids[:, :, None]

    def by_head(array):
        return (
            array.reshape(2, 4, seqs, rows, heads, HD)
            .transpose(0, 2, 4, 1, 3, 5)
            .reshape(2 * seqs, heads, length, HD)
        )

    def by_token(array):
        return (
            array.reshape(2, seqs, heads, 4, rows, HD)
            .transpose(0, 3, 1, 4, 2, 5)
            .reshape(tokens, hw)
        )

    query_rot = by_head(
        turn_heads(
            (query_pre * query_inv * query_g).reshape(tokens, heads, HD), cosine, sine
        ).astype(BF)
    )
    key_rot = by_head(
        turn_heads((key_pre * key_inv * key_g).reshape(tokens, heads, HD), cosine, sine).astype(BF)
    )
    value_heads = by_head(value_low)
    scores = (
        jnp.einsum("shqd,shkd->shqk", query_rot, key_rot, preferred_element_type=F32) * HD**-0.5
    )
    scores = jnp.where(allowed[:, None], scores, NEG_FILL)
    row_max = jnp.max(scores, axis=3, keepdims=True)
    exp_scores = jnp.exp(scores - row_max)
    probs = exp_scores / jnp.sum(exp_scores, axis=3, keepdims=True)
    probs_low = probs.astype(BF)
    attended = by_token(
        jnp.einsum("shqk,shkd->shqd", probs_low, value_heads, preferred_element_type=F32).astype(BF)
    )
    attn_rows = row_total(lambda part: dot_nt(part, out_w), attended)
    attn_inv = lax.rsqrt(jnp.mean(attn_rows * attn_rows, axis=1, keepdims=True) + EPS)
    hidden_rows = own_tokens.astype(F32) + attn_rows * attn_inv * attn_g
    mid_full = spread(hidden_rows.astype(BF))
    gate_pre = dot(mid_full, gate_w)
    up_pre = dot(mid_full, up_w)
    gate_sig = jax.nn.sigmoid(gate_pre)
    mixed = (gate_pre * gate_sig * up_pre).astype(BF)
    ffn_rows = row_total(lambda part: dot_nt(part, down_w), mixed)
    ffn_inv = lax.rsqrt(jnp.mean(ffn_rows * ffn_rows, axis=1, keepdims=True) + EPS)
    output_rows = hidden_rows + ffn_rows * ffn_inv * ffn_g

    ffn_back = norm_back(ffn_rows, ffn_inv, ffn_g, cot_rows)
    ffn_gain_part = jnp.sum(cot_rows * ffn_rows * ffn_inv, axis=0)
    ffn_back_full = spread(ffn_back.astype(BF))
    down_grad = reduce_grad(ffn_back_full, mixed)
    mixed_grad = dot(ffn_back_full, down_w)
    gate_low = (mixed_grad * up_pre * gate_sig * (1.0 + gate_pre * (1.0 - gate_sig))).astype(BF)
    up_low = (mixed_grad * gate_pre * gate_sig).astype(BF)
    gate_grad = reduce_grad(mid_full, gate_low)
    up_grad = reduce_grad(mid_full, up_low)
    units = gate_low.shape[1]

    def mid_term(part):
        return dot_nt(part[:, :units], gate_w) + dot_nt(part[:, units:], up_w)

    hidden_grad = cot_rows + row_total(mid_term, jnp.concatenate([gate_low, up_low], axis=1))
    attn_back = norm_back(attn_rows, attn_inv, attn_g, hidden_grad)
    attn_gain_part = jnp.sum(hidden_grad * attn_rows * attn_inv, axis=0)
    attn_back_full = spread(attn_back.astype(BF))
    out_grad = reduce_grad(attn_back_full, attended)
    attended_grad = by_head(dot(attn_back_full, out_w).astype(BF))
    prob_grad = jnp.einsum(
        "shqd,shkd->shqk", attended_grad, value_heads, preferred_element_type=F32
    )
    inner_sum = jnp.sum(probs * prob_grad, axis=3, keepdims=True)
    score_low = (probs * (prob_grad - inner_sum)).astype(BF)
    query_rot_grad = by_token(
        jnp.einsum("shqk,shkd->shqd", score_low, key_rot, preferred_element_type=F32) * HD**-0.5
    )
    key_rot_grad = by_token(
        jnp.einsum("shqk,shqd->shkd", score_low, query_rot, preferred_element_type=F32) * HD**-0.5
    )
    value_back = by_token(
        jnp.einsum(
            "shqk,shqd->shkd", probs_low, attended_grad, preferred_element_type=F32
        ).astype(BF)
    )
    query_norm_grad = turn_back(query_rot_grad.reshape(tokens, heads, HD), cosine, sine).reshape(
        tokens, hw
    )
    key_norm_grad = turn_back(key_rot_grad.reshape(tokens, heads, HD), cosine, sine).reshape(
        tokens, hw
    )
    query_gain_part = jnp.sum(query_norm_grad * query_pre * query_inv, axis=0)
    key_gain_part = jnp.sum(key_norm_grad * key_pre * key_inv, axis=0)
    query_scaled = query_norm_grad * query_g
    key_scaled = key_norm_grad * key_g
    dots = sum_rows(
        jnp.stack([jnp.sum(query_pre * query_scaled, axis=1), jnp.sum(key_pre * key_scaled, axis=1)])
    )
    query_dot, key_dot = dots[0][:, None], dots[1][:, None]
    query_low = (query_inv * query_scaled - query_pre * query_inv**3 * (query_dot / D)).astype(BF)
    key_low = (key_inv * key_scaled - key_pre * key_inv**3 * (key_dot / D)).astype(BF)
    qkv_low = jnp.concatenate([query_low, key_low, value_back], axis=1)
    qkv_grad = reduce_grad(tok_full, qkv_low)
    input_rows = hidden_grad + row_total(lambda part: dot_nt(part, qkv_w), qkv_low)

    def own_columns(grad):
        return by_side(grad[0], grad[1], 1).astype(F32)

    def own_thirds(grad, which):
        return own_columns([part[:, which * hw : (which + 1) * hw] for part in grad])

    def sum_dp(array):
        step = 1
        while step < dp:
            array = array + lax.ppermute(array, "dp", [(i, i ^ step) for i in range(dp)])
            step *= 2
        return array

    def placed(part):
        return lax.dynamic_update_slice(jnp.zeros((2 * hw,), F32), part, (side * hw,))

    shared = jnp.stack([attn_gain_part, ffn_gain_part])
    shared = shared + core_send(shared)
    shared = shared + y_send(shared)
    gains = sum_dp(
        jnp.concatenate(
            [placed(query_gain_part), placed(key_gain_part), shared.reshape(-1)]
        ).reshape(-1, HD)
    ).reshape(-1)
    return (
        output_rows.astype(BF).reshape(inputs.shape),
        input_rows.reshape(inputs.shape),
        own_thirds(qkv_grad, 0),
        own_thirds(qkv_grad, 1),
        own_thirds(qkv_grad, 2),
        own_columns(out_grad),
        gains[: 2 * hw],
        gains[2 * hw : 4 * hw],
        gains[4 * hw : 4 * hw + D],
        own_columns(gate_grad),
        own_columns(up_grad),
        own_columns(down_grad),
        gains[4 * hw + D :],
    )


def solution(mesh):
    whole = P()
    both = P("dp", "tensor")
    rows = P("dp", "tensor", None)
    lanes = P("tensor")
    return jax.shard_map(
        body,
        mesh=mesh,
        in_specs=(
            rows, both, both, both, both, lanes, lanes, whole, both, both, both, whole,
            P("dp", None), P("dp", None), rows,
        ),
        out_specs=(
            rows, rows, both, both, both, both, lanes, lanes, whole, both, both, both, whole,
        ),
        check_vma=False,
    )
```

time: 1180 us -> 1140 us (0.966)
  other arithmetic: 82 us -> 238 us
  matrix products: 320 us -> 225 us
  starting transfers between devices: 140 us -> 56.4 us
  blocking collectives: 58.5 us -> 22.1 us
  between operations: 3.61 us -> 16.4 us
    concatenate x14 -> x25, other arithmetic: 24 us -> 142 us  [the longest x4 121 us: spread(): even = jnp.concatenate([low, high], axis=1)]
    ppermute x84 -> x49, waiting for transfers between devices: 414 us -> 311 us  [the longest x29 192 us: x_send(): return lax.ppermute(array, 'dp', x_perm)]
    ppermute x84 -> x49, starting transfers between devices: 137 us -> 54.6 us  [the longest x29 34.3 us: x_send(): return lax.ppermute(array, 'dp', x_perm)]
    all_gather x0 -> x5, waiting for transfers between devices: none -> 77.7 us  [gather(): lax.all_gather(by_side(mine, other, 0), 'dp', axis=0, tiled=True, axis_in...]
    psum x3 -> x2, blocking collectives: 58.5 us -> 22.1 us  [sum_rows(): parts = lax.psum(parts, 'tensor')]
    dot_general x24 -> x10, matrix products: 107 us -> 70.5 us  [dot_nt(): lax.dot_general(left, right, (((1,), (1,)), ((), ())), preferred_element_...]
    dot_general x5, matrix products: 102 us -> 66.5 us  [dot(): return jnp.dot(left, right, preferred_element_type=F32)]
    dot_general x40 -> x5, matrix products: 88.4 us -> 57.1 us  [dot_tn(): lax.dot_general(left, right, (((0,), (0,)), ((), ())), preferred_element_...]
  transfers between devices with their start and end apart: 105 -> 68, of which waited for: 48 -> 37; matrix products, arithmetic and copies ran while one was open for 41% -> 41% of each run, Pallas kernels for 0% -> 0%
where the time goes in v2:
time: 1140 us; the launch traced here: 1130 us
  waiting for transfers between devices  407 us (36%)
  other arithmetic  238 us (21%)
  matrix products  225 us (20%)
  local copies, waits for them, and re-layouts  160 us (14%)
  starting transfers between devices  56.4 us (5%)
  blocking collectives  22.1 us (2%)
  between operations  16.4 us (1%)
    ppermute x29, waiting for transfers between devices, x_send(): return lax.ppermute(array, 'dp', x_perm)  192 us
    concatenate x4, other arithmetic, spread(): even = jnp.concatenate([low, high], axis=1)  121 us
    ppermute x17, waiting for transfers between devices, y_send(): return lax.ppermute(array, 'tensor', y_perm)  115 us
    all_gather x5, waiting for transfers between devices, gather(): lax.all_gather(by_side(mine, other, 0), 'dp', axis=0, tiled=True, axis_in...  77.7 us
    unnamed x214, local copies, waits for them, and re-layouts  71.3 us
    dot_general x10, matrix products, dot_nt(): lax.dot_general(left, right, (((1,), (1,)), ((), ())), preferred_element_...  70.5 us
    dot_general x5, matrix products, dot(): return jnp.dot(left, right, preferred_element_type=F32)  66.5 us
    dot_general x5, matrix products, dot_tn(): lax.dot_general(left, right, (((0,), (0,)), ((), ())), preferred_element_...  57.1 us
  transfers between devices with their start and end apart: 68, of which 37 were waited for; matrix products, arithmetic and copies ran while one was open for 41% of the time, Pallas kernels for 0%

profile of v2, /device:TPU:0, one launch (start us, length us, event | category | flops | bytes accessed | tf_op | source)
XLA Modules:
  0.0 1125.5 jit_solution(8700269951922038271)
XLA Ops:
  13.0 10.4 collective-permute-done.1
  27.0 20.9 %collective-permute-done.2 = bf16[512,1024]{1,0:T(8,128)(2,1)S(1)} collective-permute-done((bf16[512,1024]{1,0:T(8,128)(2,1)S(1)}, bf16[512,1024]{1,0:T(8,128)(2,1)S(1)}, u32[]{:S(2)}, u32[]{:S(2)}) %collective-permute-start.2) | collective-permute-done | bytes 1048608 | tf_op jit(solution)/shard_map/ppermute | solution.py:96
  49.3 30.2 %maximum_maximum_fusion = bf16[1024,2048]{1,0:T(8,128)(2,1)} fusion(bf16[512,1024]{1,0:T(8,128)(2,1)S(1)} %collective-permute-done.4, bf16[256,1024]{1,0:T(8,128)(2,1)S(1)} %collective-permute-done.3, bf16[256,1024]{1,0:T(8,128)(2,1)S(1)} %get-tuple-element.118, bf16[256,1024]{1,0:T(8,128)(2,1)S(1)} %get-tuple-element.116, ...), kind=kLoop, calls=%fused_computation.34 | loop fusion | flops 29360128 | bytes 8388608 | tf_op jit(solution)/shard_map/concatenate | solution.py:150
  83.6 10.5 collective-permute-done
  97.4 15.4 %fusion.88 = (f32[2,4,2,128,128]{3,2,1,0,4:T(2,128)S(1)}, f32[2,4,2,128,128]{3,2,1,0,4:T(2,128)}) fusion(f32[2,4,2,128,64]{3,2,1,0,4:T(2,128)S(1)} %broadcast_multiply_fusion.3), kind=kLoop, calls=%fused_computation.243 | loop fusion | flops 262144 | bytes 2621440 | tf_op jit(solution)/shard_map/cos | solution.py:35
  131.5 27.8 %all-gather.6.cloned.1.call-done = bf16[2048,768]{1,0:T(8,128)(2,1)} async-done(((bf16[512,768]{1,0:T(8,128)(2,1)}), bf16[2048,768]{1,0:T(8,128)(2,1)}) %all-gather.6.cloned.1.call-update) | async-done | bytes 3145744 | tf_op jit(solution)/shard_map/all_gather | solution.py:117
  159.3 10.4 fusion.140
  173.0 11.2 psum.14
  251.3 13.8 %collective-permute-done.19 = bf16[256,1024]{1,0:T(8,128)(2,1)} collective-permute-done((bf16[256,1024]{1,0:T(8,128)(2,1)S(1)}, bf16[256,1024]{1,0:T(8,128)(2,1)}, u32[]{:S(2)}, u32[]{:S(2)}) %collective-permute-start.19) | collective-permute-done | bytes 524320 | tf_op jit(solution)/shard_map/ppermute | solution.py:93
  274.9 22.3 %collective-permute-done.10 = bf16[512,1024]{1,0:T(8,128)(2,1)S(1)} collective-permute-done((bf16[512,1024]{1,0:T(8,128)(2,1)S(1)}, bf16[512,1024]{1,0:T(8,128)(2,1)S(1)}, u32[]{:S(2)}, u32[]{:S(2)}) %collective-permute-start.10) | collective-permute-done | bytes 1048608 | tf_op jit(solution)/shard_map/ppermute | solution.py:93
  308.4 11.2 collective-permute-done.20
  333.9 10.3 collective-permute-done.14
  348.6 19.6 %collective-permute-done.15 = bf16[512,1024]{1,0:T(8,128)(2,1)S(1)} collective-permute-done((bf16[512,1024]{1,0:T(8,128)(2,1)S(1)}, bf16[512,1024]{1,0:T(8,128)(2,1)S(1)}, u32[]{:S(2)}, u32[]{:S(2)}) %collective-permute-start.15) | collective-permute-done | bytes 1048608 | tf_op jit(solution)/shard_map/ppermute | solution.py:96
  368.8 30.6 %maximum_maximum_fusion.1 = bf16[1024,2048]{1,0:T(8,128)(2,1)} fusion(bf16[512,1024]{1,0:T(8,128)(2,1)S(1)} %collective-permute-done.17, bf16[256,1024]{1,0:T(8,128)(2,1)S(1)} %collective-permute-done.16, bf16[256,1024]{1,0:T(8,128)(2,1)S(1)} %get-tuple-element.106, bf16[256,1024]{1,0:T(8,128)(2,1)S(1)} %get-tuple-element.104, ...), kind=kLoop, calls=%fused_computation.35 | loop fusion | flops 29360128 | bytes 8388608 | tf_op jit(solution)/shard_map/concatenate | solution.py:150
  423.1 14.7 %fusion.141 = f32[2048,1024]{1,0:T(8,128)} fusion(bf16[2048,2048]{1,0:T(8,128)(2,1)} %slice_dynamic-update-slice_fusion.16, bf16[2048,1024]{1,0:T(8,128)(2,1)} %all-gather.10.cloned.1.call-done), kind=kOutput, calls=%fused_computation.377 | convolution fusion | flops 8589934592 | bytes 20971520 | tf_op jit(solution)/shard_map/dot_general | solution.py:16
  437.8 16.3 %multiply_convert_fusion.3 = (bf16[2048,1024]{1,0:T(8,128)(2,1)S(1)}, f32[2048,1024]{1,0:T(8,128)}) fusion(f32[2048,1024]{1,0:T(8,128)} %fusion.141, bf16[2048,2048]{1,0:T(8,128)(2,1)} %slice_dynamic-update-slice_fusion.16, bf16[2048,1024]{1,0:T(8,128)(2,1)} %all-gather.12.cloned.1.call-done), kind=kOutput, calls=%fused_computation.26 | convolution fusion | flops 8602517504 | bytes 33554432 | tf_op jit(solution)/shard_map/dot_general | solution.py:16
  457.5 49.9 %all-gather.14.cloned.1.call-done = bf16[2048,1024]{1,0:T(8,128)(2,1)} async-done(((bf16[512,1024]{1,0:T(8,128)(2,1)}), bf16[2048,1024]{1,0:T(8,128)(2,1)}) %all-gather.14.cloned.1.call-update) | async-done | bytes 4194320 | tf_op jit(solution)/shard_map/all_gather | solution.py:117
  536.4 22.1 %collective-permute-done.25 = bf16[512,1024]{1,0:T(8,128)(2,1)S(1)} collective-permute-done((bf16[512,1024]{1,0:T(8,128)(2,1)S(1)}, bf16[512,1024]{1,0:T(8,128)(2,1)S(1)}, u32[]{:S(2)}, u32[]{:S(2)}) %collective-permute-start.25) | collective-permute-done | bytes 1048608 | tf_op jit(solution)/shard_map/ppermute | solution.py:96
  590.4 20.6 %collective-permute-done.28 = bf16[512,1024]{1,0:T(8,128)(2,1)S(1)} collective-permute-done((bf16[512,1024]{1,0:T(8,128)(2,1)S(1)}, bf16[512,1024]{1,0:T(8,128)(2,1)S(1)}, u32[]{:S(2)}, u32[]{:S(2)}) %collective-permute-start.28) | collective-permute-done | bytes 1048608 | tf_op jit(solution)/shard_map/ppermute | solution.py:96
  611.5 29.5 %maximum_maximum_fusion.2 = bf16[1024,2048]{1,0:T(8,128)(2,1)S(1)} fusion(bf16[512,1024]{1,0:T(8,128)(2,1)S(1)} %collective-permute-done.30, bf16[256,1024]{1,0:T(8,128)(2,1)S(1)} %collective-permute-done.29, bf16[256,1024]{1,0:T(8,128)(2,1)S(1)} %get-tuple-element.102, bf16[256,1024]{1,0:T(8,128)(2,1)S(1)} %get-tuple-element.100, ...), kind=kLoop, calls=%fused_computation.36 | loop fusion | flops 29360128 | bytes 8388608 | tf_op jit(solution)/shard_map/concatenate | solution.py:150
  652.2 18.4 %multiply_convert_fusion.2 = (bf16[2048,1024]{1,0:T(8,128)(2,1)S(1)}, bf16[2048,1024]{1,0:T(8,128)(2,1)S(1)}) fusion(f32[2048,1024]{1,0:T(8,128)} %fusion.141, f32[2048,1024]{1,0:T(8,128)} %get-tuple-element.156, bf16[2048,2048]{1,0:T(8,128)(2,1)} %copy-done.55, bf16[2048,1024]{1,0:T(8,128)(2,1)} %all-gather.14.cloned.1.call-done), kind=kOutput, calls=%fused_computation.24 | convolution fusion | flops 8617197568 | bytes 37748736 | tf_op jit(solution)/shard_map/dot_general | solution.py:16
  696.6 12.7 %convolution_convert_fusion.5 = bf16[2048,1024]{1,0:T(8,128)(2,1)} fusion(bf16[2048,2048]{1,0:T(8,128)(2,1)} %slice_dynamic-update-slice_fusion.16, bf16[2048,1024]{1,0:T(8,128)(2,1)S(1)} %get-tuple-element.27), kind=kOutput, calls=%fused_computation.48 | convolution fusion | flops 8592031744 | bytes 16777216 | tf_op jit(solution)/shard_map/dot_general | solution.py:24
  719.4 11.0 fusion.138
  733.7 22.3 %collective-permute-done.33 = bf16[512,1024]{1,0:T(8,128)(2,1)S(1)} collective-permute-done((bf16[512,1024]{1,0:T(8,128)(2,1)S(1)}, bf16[512,1024]{1,0:T(8,128)(2,1)S(1)}, u32[]{:S(2)}, u32[]{:S(2)}) %collective-permute-start.33) | collective-permute-done | bytes 1048608 | tf_op jit(solution)/shard_map/ppermute | solution.py:93
  760.7 12.8 %convolution_convert_fusion.4 = bf16[2048,1024]{1,0:T(8,128)(2,1)} fusion(bf16[2048,2048]{1,0:T(8,128)(2,1)} %slice_dynamic-update-slice_fusion.16, bf16[2048,1024]{1,0:T(8,128)(2,1)S(1)} %copy-done.12), kind=kOutput, calls=%fused_computation.47 | convolution fusion | flops 8592031744 | bytes 16777216 | tf_op jit(solution)/shard_map/dot_general | solution.py:24
  796.0 10.4 collective-permute-done.37
  808.7 21.4 %collective-permute-done.38 = bf16[512,1024]{1,0:T(8,128)(2,1)S(1)} collective-permute-done((bf16[512,1024]{1,0:T(8,128)(2,1)S(1)}, bf16[512,1024]{1,0:T(8,128)(2,1)S(1)}, u32[]{:S(2)}, u32[]{:S(2)}) %collective-permute-start.38) | collective-permute-done | bytes 1048608 | tf_op jit(solution)/shard_map/ppermute | solution.py:96
  830.3 30.4 %maximum_maximum_fusion.3 = bf16[1024,2048]{1,0:T(8,128)(2,1)} fusion(bf16[512,1024]{1,0:T(8,128)(2,1)S(1)} %collective-permute-done.40, bf16[256,1024]{1,0:T(8,128)(2,1)S(1)} %collective-permute-done.39, bf16[256,1024]{1,0:T(8,128)(2,1)S(1)} %get-tuple-element.98, bf16[256,1024]{1,0:T(8,128)(2,1)S(1)} %get-tuple-element.96, ...), kind=kLoop, calls=%fused_computation.38 | loop fusion | flops 29360128 | bytes 8388608 | tf_op jit(solution)/shard_map/concatenate | solution.py:150
  865.4 14.2 %convolution_convert_fusion.3 = bf16[2048,1024]{1,0:T(8,128)(2,1)} fusion(bf16[2048,2048]{1,0:T(8,128)(2,1)} %copy-done.55, bf16[2048,1024]{1,0:T(8,128)(2,1)} %copy-done.28), kind=kOutput, calls=%fused_computation.46 | convolution fusion | flops 8592031744 | bytes 16777216 | tf_op jit(solution)/shard_map/dot_general | solution.py:24
  965.4 11.0 psum.15
  1007.1 10.5 convolution_convert_fusion.6
  1071.5 18.1 %collective-permute-done.44 = bf16[512,1024]{1,0:T(8,128)(2,1)S(1)} collective-permute-done((bf16[512,1024]{1,0:T(8,128)(2,1)}, bf16[512,1024]{1,0:T(8,128)(2,1)S(1)}, u32[]{:S(2)}, u32[]{:S(2)}) %collective-permute-start.44) | collective-permute-done | bytes 1048608 | tf_op jit(solution)/shard_map/ppermute | solution.py:93
  (563 shorter events, 518.3 us)
Async XLA Ops:
  7.2 152.1 %all-gather.6.cloned.1.call-start = ((), (), s32[]{:S(2)}) async-start(), calls=%async_computation.5 | async-start | bytes 3932160 | tf_op jit(solution)/shard_map/all_gather | solution.py:117
  23.5 24.4 %collective-permute-start.2 = (bf16[512,1024]{1,0:T(8,128)(2,1)S(1)}, bf16[512,1024]{1,0:T(8,128)(2,1)S(1)}, u32[]{:S(2)}, u32[]{:S(2)}) collective-permute-start(bf16[512,1024]{1,0:T(8,128)(2,1)S(1)} %pad_maximum_fusion.8), channel_id=1, source_target_pairs={{0,2},{1,3},{2,0},{3,1},{4,6},{5,7},{6,4},{7,5},{8,10},{9,11},{10,... | collective-permute-start | bytes 3145736 | tf_op jit(solution)/shard_map/ppermute | solution.py:96
  25.4 23.8 %collective-permute-start.4 = (bf16[512,1024]{1,0:T(8,128)(2,1)S(1)}, bf16[512,1024]{1,0:T(8,128)(2,1)S(1)}, u32[]{:S(2)}, u32[]{:S(2)}) collective-permute-start(bf16[512,1024]{1,0:T(8,128)(2,1)S(1)} %pad_maximum_fusion.9), channel_id=1, source_target_pairs={{0,4},{4,0},{8,12},{12,8},{16,20},{20,16},{24,28},{28,24},{1,5},{5... | collective-permute-start | bytes 3145736 | tf_op jit(solution)/shard_map/ppermute | solution.py:93
  79.5 35.7 %collective-permute-start.5 = (bf16[1024,2048]{1,0:T(8,128)(2,1)}, bf16[1024,2048]{1,0:T(8,128)(2,1)}, u32[]{:S(2)}, u32[]{:S(2)}) collective-permute-start(bf16[1024,2048]{1,0:T(8,128)(2,1)} %maximum_maximum_fusion), channel_id=1, source_target_pairs={{0,1},{1,0},{2,3},{3,2},{4,5},{5,4},{6,7},{7,6},{8,9},{9,8},{10,11... | collective-permute-start | bytes 12582920 | tf_op jit(solution)/shard_map/ppermute | solution.py:99
  79.5 33.3 %collective-permute-start.8 = (bf16[256,256]{1,0:T(8,128)(2,1)S(1)}, bf16[256,256]{1,0:T(8,128)(2,1)S(1)}, u32[]{:S(2)}, u32[]{:S(2)}) collective-permute-start(bf16[256,256]{1,0:T(8,128)(2,1)S(1)} %constant_dynamic-slice_fusion.8), channel_id=1, source_target_pairs={{0,4},{4,0},{8,12},{12,8},{16,20},{20,16},{24,28},{28,24},{1,5},{5... | collective-permute-start | bytes 393224 | tf_op jit(solution)/shard_map/ppermute | solution.py:93
  95.3 150.4 %all-gather.8.cloned.1.call-start = ((), (), s32[]{:S(2)}) async-start(), calls=%async_computation.6 | async-start | bytes 1310720 | tf_op jit(solution)/shard_map/all_gather | solution.py:117
  186.4 236.7 %all-gather.10.cloned.1.call-start = ((), (), s32[]{:S(2)}) async-start(), calls=%async_computation.7 | async-start | bytes 5242880 | tf_op jit(solution)/shard_map/all_gather | solution.py:117
  267.4 170.4 %all-gather.12.cloned.1.call-start = ((), (), s32[]{:S(2)}) async-start(), calls=%async_computation.8 | async-start | bytes 5242880 | tf_op jit(solution)/shard_map/all_gather | solution.py:117
  271.1 26.1 %collective-permute-start.10 = (bf16[512,1024]{1,0:T(8,128)(2,1)S(1)}, bf16[512,1024]{1,0:T(8,128)(2,1)S(1)}, u32[]{:S(2)}, u32[]{:S(2)}) collective-permute-start(bf16[512,1024]{1,0:T(8,128)(2,1)S(1)} %slice.707), channel_id=1, source_target_pairs={{0,4},{4,0},{8,12},{12,8},{16,20},{20,16},{24,28},{28,24},{1,5},{5... | collective-permute-start | bytes 3145736 | tf_op jit(solution)/shard_map/ppermute | solution.py:93
  272.0 26.4 %collective-permute-start.12 = (bf16[512,1024]{1,0:T(8,128)(2,1)S(1)}, bf16[512,1024]{1,0:T(8,128)(2,1)S(1)}, u32[]{:S(2)}, u32[]{:S(2)}) collective-permute-start(bf16[512,1024]{1,0:T(8,128)(2,1)S(1)} %pad_maximum_fusion.11), channel_id=1, source_target_pairs={{0,2},{1,3},{2,0},{3,1},{4,6},{5,7},{6,4},{7,5},{8,10},{9,11},{10,... | collective-permute-start | bytes 3145736 | tf_op jit(solution)/shard_map/ppermute | solution.py:96
  272.7 35.8 %collective-permute-start.21 = (bf16[256,1024]{1,0:T(8,128)(2,1)S(1)}, bf16[256,1024]{1,0:T(8,128)(2,1)S(1)}, u32[]{:S(2)}, u32[]{:S(2)}) collective-permute-start(bf16[256,1024]{1,0:T(8,128)(2,1)S(1)} %constant_dynamic-slice_fusion.5), channel_id=1, source_target_pairs={{0,4},{4,0},{8,12},{12,8},{16,20},{20,16},{24,28},{28,24},{1,5},{5... | collective-permute-start | bytes 1572872 | tf_op jit(solution)/shard_map/ppermute | solution.py:93
  274.2 45.4 %collective-permute-start.20 = (bf16[256,1024]{1,0:T(8,128)(2,1)S(1)}, bf16[256,1024]{1,0:T(8,128)(2,1)S(1)}, u32[]{:S(2)}, u32[]{:S(2)}) collective-permute-start(bf16[256,1024]{1,0:T(8,128)(2,1)S(1)} %constant_dynamic-slice_fusion.6), channel_id=1, source_target_pairs={{0,4},{4,0},{8,12},{12,8},{16,20},{20,16},{24,28},{28,24},{1,5},{5... | collective-permute-start | bytes 1572872 | tf_op jit(solution)/shard_map/ppermute | solution.py:93
  298.5 31.1 %collective-permute-start.13 = (bf16[256,1024]{1,0:T(8,128)(2,1)S(1)}, bf16[256,1024]{1,0:T(8,128)(2,1)S(1)}, u32[]{:S(2)}, u32[]{:S(2)}) collective-permute-start(bf16[256,1024]{1,0:T(8,128)(2,1)S(1)} %fusion.79), channel_id=1, source_target_pairs={{0,4},{4,0},{8,12},{12,8},{16,20},{20,16},{24,28},{28,24},{1,5},{5... | collective-permute-start | bytes 1572872 | tf_op jit(solution)/shard_map/ppermute | solution.py:93
  333.2 174.2 %all-gather.14.cloned.1.call-start = ((), (), s32[]{:S(2)}) async-start(), calls=%async_computation.9 | async-start | bytes 5242880 | tf_op jit(solution)/shard_map/all_gather | solution.py:117
  344.3 24.0 %collective-permute-start.15 = (bf16[512,1024]{1,0:T(8,128)(2,1)S(1)}, bf16[512,1024]{1,0:T(8,128)(2,1)S(1)}, u32[]{:S(2)}, u32[]{:S(2)}) collective-permute-start(bf16[512,1024]{1,0:T(8,128)(2,1)S(1)} %pad_maximum_fusion.12), channel_id=1, source_target_pairs={{0,2},{1,3},{2,0},{3,1},{4,6},{5,7},{6,4},{7,5},{8,10},{9,11},{10,... | collective-permute-start | bytes 3145736 | tf_op jit(solution)/shard_map/ppermute | solution.py:96
  400.5 483.3 %reduce-scatter.10.cloned.1.call-start = ((), (), s32[]{:S(2)}) async-start(), calls=%async_computation.12 | async-start | bytes 5242880 | tf_op jit(solution)/shard_map/reduce_scatter | solution.py:122
  533.2 25.3 %collective-permute-start.25 = (bf16[512,1024]{1,0:T(8,128)(2,1)S(1)}, bf16[512,1024]{1,0:T(8,128)(2,1)S(1)}, u32[]{:S(2)}, u32[]{:S(2)}) collective-permute-start(bf16[512,1024]{1,0:T(8,128)(2,1)S(1)} %pad_maximum_fusion.17), channel_id=1, source_target_pairs={{0,2},{1,3},{2,0},{3,1},{4,6},{5,7},{6,4},{7,5},{8,10},{9,11},{10,... | collective-permute-start | bytes 3145736 | tf_op jit(solution)/shard_map/ppermute | solution.py:96
  534.9 25.3 %collective-permute-start.23 = (bf16[512,1024]{1,0:T(8,128)(2,1)S(1)}, bf16[512,1024]{1,0:T(8,128)(2,1)S(1)}, u32[]{:S(2)}, u32[]{:S(2)}) collective-permute-start(bf16[512,1024]{1,0:T(8,128)(2,1)S(1)} %slice.737), channel_id=1, source_target_pairs={{0,4},{4,0},{8,12},{12,8},{16,20},{20,16},{24,28},{28,24},{1,5},{5... | collective-permute-start | bytes 3145736 | tf_op jit(solution)/shard_map/ppermute | solution.py:93
  709.4 310.6 %reduce-scatter.12.cloned.1.call-start = ((), (), s32[]{:S(2)}) async-start(), calls=%async_computation.13 | async-start | bytes 5242880 | tf_op jit(solution)/shard_map/reduce_scatter | solution.py:122
  730.5 25.5 %collective-permute-start.33 = (bf16[512,1024]{1,0:T(8,128)(2,1)S(1)}, bf16[512,1024]{1,0:T(8,128)(2,1)S(1)}, u32[]{:S(2)}, u32[]{:S(2)}) collective-permute-start(bf16[512,1024]{1,0:T(8,128)(2,1)S(1)} %slice.777), channel_id=1, source_target_pairs={{0,4},{4,0},{8,12},{12,8},{16,20},{20,16},{24,28},{28,24},{1,5},{5... | collective-permute-start | bytes 3145736 | tf_op jit(solution)/shard_map/ppermute | solution.py:93
  732.2 41.5 %collective-permute-start.35 = (bf16[512,1024]{1,0:T(8,128)(2,1)}, bf16[512,1024]{1,0:T(8,128)(2,1)}, u32[]{:S(2)}, u32[]{:S(2)}) collective-permute-start(bf16[512,1024]{1,0:T(8,128)(2,1)} %pad_maximum_fusion.20), channel_id=1, source_target_pairs={{0,2},{1,3},{2,0},{3,1},{4,6},{5,7},{6,4},{7,5},{8,10},{9,11},{10,... | collective-permute-start | bytes 3145736 | tf_op jit(solution)/shard_map/ppermute | solution.py:96
  773.5 250.3 %reduce-scatter.14.cloned.1.call-start = ((), (), s32[]{:S(2)}) async-start(), calls=%async_computation.14 | async-start | bytes 5242880 | tf_op jit(solution)/shard_map/reduce_scatter | solution.py:122
  806.4 23.6 %collective-permute-start.38 = (bf16[512,1024]{1,0:T(8,128)(2,1)S(1)}, bf16[512,1024]{1,0:T(8,128)(2,1)S(1)}, u32[]{:S(2)}, u32[]{:S(2)}) collective-permute-start(bf16[512,1024]{1,0:T(8,128)(2,1)S(1)} %pad_maximum_fusion.21), channel_id=1, source_target_pairs={{0,2},{1,3},{2,0},{3,1},{4,6},{5,7},{6,4},{7,5},{8,10},{9,11},{10,... | collective-permute-start | bytes 3145736 | tf_op jit(solution)/shard_map/ppermute | solution.py:96
  860.7 26.1 %collective-permute-start.41 = (bf16[1024,2048]{1,0:T(8,128)(2,1)}, bf16[1024,2048]{1,0:T(8,128)(2,1)}, u32[]{:S(2)}, u32[]{:S(2)}) collective-permute-start(bf16[1024,2048]{1,0:T(8,128)(2,1)} %maximum_maximum_fusion.3), channel_id=1, source_target_pairs={{0,1},{1,0},{2,3},{3,2},{4,5},{5,4},{6,7},{7,6},{8,9},{9,8},{10,11... | collective-permute-start | bytes 12582920 | tf_op jit(solution)/shard_map/ppermute | solution.py:99
  879.7 190.3 %reduce-scatter.8.cloned.1.call-start = ((), (), s32[]{:S(2)}) async-start(), calls=%async_computation.11 | async-start | bytes 1310720 | tf_op jit(solution)/shard_map/reduce_scatter | solution.py:122
  881.0 136.6 %collective-permute-start.50 = (f32[2,2048]{1,0:T(2,128)}, f32[2,2048]{1,0:T(2,128)}, u32[]{:S(2)}, u32[]{:S(2)}) collective-permute-start(f32[2,2048]{1,0:T(2,128)} %pad_maximum_fusion.29), channel_id=1, source_target_pairs={{0,1},{1,0},{2,3},{3,2},{4,5},{5,4},{6,7},{7,6},{8,9},{9,8},{10,11... | collective-permute-start | bytes 49160 | tf_op jit(solution)/shard_map/ppermute | solution.py:99
  885.7 141.3 %collective-permute-start.55 = (bf16[256,1024]{1,0:T(8,128)(2,1)}, bf16[256,1024]{1,0:T(8,128)(2,1)}, u32[]{:S(2)}, u32[]{:S(2)}) collective-permute-start(bf16[256,1024]{1,0:T(8,128)(2,1)} %constant_dynamic-slice_fusion.2), channel_id=1, source_target_pairs={{0,4},{4,0},{8,12},{12,8},{16,20},{20,16},{24,28},{28,24},{1,5},{5... | collective-permute-start | bytes 1572872 | tf_op jit(solution)/shard_map/ppermute | solution.py:93
  993.9 112.9 %reduce-scatter.6.cloned.1.call-start = ((), (), s32[]{:S(2)}) async-start(), calls=%async_computation.10 | async-start | bytes 3932160 | tf_op jit(solution)/shard_map/reduce_scatter | solution.py:122
  1007.1 47.7 %collective-permute-start.43 = (bf16[1024,2048]{1,0:T(8,128)(2,1)}, bf16[1024,2048]{1,0:T(8,128)(2,1)}, u32[]{:S(2)}, u32[]{:S(2)}) collective-permute-start(bf16[1024,2048]{1,0:T(8,128)(2,1)} %convolution_convert_fusion.1), channel_id=1, source_target_pairs={{0,1},{1,0},{2,3},{3,2},{4,5},{5,4},{6,7},{7,6},{8,9},{9,8},{10,11... | collective-permute-start | bytes 12582920 | tf_op jit(solution)/shard_map/ppermute | solution.py:99
  1063.7 25.9 %collective-permute-start.44 = (bf16[512,1024]{1,0:T(8,128)(2,1)}, bf16[512,1024]{1,0:T(8,128)(2,1)S(1)}, u32[]{:S(2)}, u32[]{:S(2)}) collective-permute-start(bf16[512,1024]{1,0:T(8,128)(2,1)} %slice.813), channel_id=1, source_target_pairs={{0,4},{4,0},{8,12},{12,8},{16,20},{20,16},{24,28},{28,24},{1,5},{5... | collective-permute-start | bytes 3145736 | tf_op jit(solution)/shard_map/ppermute | solution.py:93
  1065.6 26.1 %collective-permute-start.46 = (bf16[512,1024]{1,0:T(8,128)(2,1)}, bf16[512,1024]{1,0:T(8,128)(2,1)}, u32[]{:S(2)}, u32[]{:S(2)}) collective-permute-start(bf16[512,1024]{1,0:T(8,128)(2,1)} %pad_maximum_fusion.24), channel_id=1, source_target_pairs={{0,2},{1,3},{2,0},{3,1},{4,6},{5,7},{6,4},{7,5},{8,10},{9,11},{10,... | collective-permute-start | bytes 3145736 | tf_op jit(solution)/shard_map/ppermute | solution.py:96
  1070.9 23.5 %collective-permute-start.49 = (bf16[256,256]{1,0:T(8,128)(2,1)S(1)}, bf16[256,256]{1,0:T(8,128)(2,1)S(1)}, u32[]{:S(2)}, u32[]{:S(2)}) collective-permute-start(bf16[256,256]{1,0:T(8,128)(2,1)S(1)} %constant_dynamic-slice_fusion.3), channel_id=1, source_target_pairs={{0,4},{4,0},{8,12},{12,8},{16,20},{20,16},{24,28},{28,24},{1,5},{5... | collective-permute-start | bytes 393224 | tf_op jit(solution)/shard_map/ppermute | solution.py:93
  (125 other events, 1694.2 us)
Sparse Core Ops, SparseCore 0:
  95.5 63.8 all-gather.5
  186.5 24.7 all-gather.7
  267.5 77.7 all-gather.9
  347.3 79.2 all-gather.11
  428.0 79.2 all-gather.13
  709.5 74.4 reduce-scatter.9
  786.4 77.2 reduce-scatter.11
  879.8 74.5 reduce-scatter.13
  994.0 24.6 reduce-scatter.7
  1020.9 59.6 reduce-scatter.5

commit v3 on v2

v3 whole, which is shorter than its diff:
```python
import jax
import jax.numpy as jnp
from jax import lax
from jax.experimental import pallas as pl
from jax.experimental.pallas import tpu as pltpu
from jax.sharding import PartitionSpec as P

D = 2048
HD = 128
EPS = 1e-06
THETA = 500000.0
NEG_FILL = -1e30
BF = jnp.bfloat16
F32 = jnp.float32


def dot(left, right):
    return jnp.dot(left, right, preferred_element_type=F32)


def dot_nt(left, right):
    return lax.dot_general(left, right, (((1,), (1,)), ((), ())), preferred_element_type=F32)


def dot_tn(left, right):
    return lax.dot_general(left, right, (((0,), (0,)), ((), ())), preferred_element_type=F32)


def after(array, others):
    return lax.optimization_barrier((array, others))[0]


def rope_tables(position_ids):
    inv_freq = 1.0 / THETA ** (jnp.arange(0, HD, 2, dtype=F32) / HD)
    angles = position_ids.astype(F32)[:, None] * inv_freq[None, :]
    angles = jnp.concatenate([angles, angles], axis=1)
    return (jnp.cos(angles), jnp.sin(angles))


MESH = pl.DeviceIdType.MESH
SCALE = HD**-0.5


def place():
    d, t = lax.axis_index("dp"), lax.axis_index("tensor")
    side, high, low = d % 2, t // 2, t % 2
    partners = ({"dp": d + 1 - 2 * side}, {"tensor": t + 2 - 4 * high}, {"tensor": t + 1 - 2 * low})
    return side, high, low, t, partners


def greet(partners):
    barrier = pltpu.get_barrier_semaphore()
    for partner in partners:
        pl.semaphore_signal(barrier, inc=1, device_id=partner, device_id_type=MESH)
    pl.semaphore_wait(barrier, len(partners))


def remote(src, dst, send_sem, recv_sem, slot, partner):
    return pltpu.make_async_remote_copy(
        src_ref=src,
        dst_ref=dst,
        send_sem=send_sem.at[slot],
        recv_sem=recv_sem.at[slot],
        device_id=partner,
        device_id_type=MESH,
    )


def spread_kernel(own, out, own_sem, send_sem, recv_sem):
    side, high, low, t, partners = place()
    x_peer, y_peer, c_peer = partners
    t_y, other = t + 2 - 4 * high, 1 - side
    width = own.shape[2] // 4

    def part(a, b, i):
        return out.at[a, :, b, :, pl.ds(i * width, width)]

    greet(partners)

    def send(src, dst, slot, peer):
        copy = remote(src, dst, send_sem, recv_sem, slot, peer)
        copy.start()
        return copy

    def own_part(i):
        return own.at[:, :, pl.ds(i * width, width)]

    x_own, y_own = {}, {}
    for i, j in ((0, 2), (1, 3), (2, 0), (3, 1)):
        x_own[i] = send(own_part(i), part(side, t, i), i, x_peer)
        y_own[j] = send(own_part(j), part(side, t, j), 4 + j, y_peer)
    copies = list(x_own.values()) + list(y_own.values())
    core = [send(own, out.at[side, :, t], 12, c_peer)]
    local = pltpu.make_async_copy(own, out.at[side, :, t], own_sem)
    local.start()
    far = {}

    def to_core(a, b, i, slot):
        core.append(send(part(a, b, i), part(a, b, i), slot, c_peer))

    for i, j in ((0, 2), (1, 3)):
        x_own[i].wait_recv()
        far[i] = send(part(other, t, i), part(other, t, i), 8 + i, y_peer)
        to_core(other, t, i, 13 + i)
        y_own[j].wait_recv()
        far[j] = send(part(side, t_y, j), part(side, t_y, j), 8 + j, x_peer)
        to_core(side, t_y, j, 17 + j)
    for i, j in ((2, 0), (3, 1)):
        x_own[i].wait_recv()
        to_core(other, t, i, 13 + i)
        y_own[j].wait_recv()
        to_core(side, t_y, j, 17 + j)
    for i in (0, 2, 1, 3):
        far[i].wait_recv()
        to_core(other, t_y, i, 21 + i)
    for copy in core:
        copy.wait_recv()
    local.wait()
    for copy in copies + list(far.values()) + core:
        copy.wait_send()


def total_kernel(
    part, out, keep, from_core, x_in, y_in, x_last, y_last, local_sem, send_sem, recv_sem
):
    side, high, low, t, partners = place()
    x_peer, y_peer, c_peer = partners
    seqs, rows, width = out.shape
    half = width // 2
    first, second = pl.ds(0, half), pl.ds(half, half)
    greet(partners)

    def send(src, dst, slot, peer):
        copy = remote(src, dst, send_sem, recv_sem, slot, peer)
        copy.start()
        return copy

    core, local = {}, {}
    order = ((1, 1), (1, 0), (0, 1), (0, 0))
    for n, (ra, ry) in enumerate(order):
        a, b = (side + ra) % 2, 2 * ((high + ry) % 2)
        for s in range(seqs):
            core[ra, ry, s] = send(
                part.at[a, s, b + 1 - low], from_core.at[ra, ry, s], n * seqs + s, c_peer
            )
            local[ra, ry, s] = pltpu.make_async_copy(
                part.at[a, s, b + low], keep.at[ra, ry, s], local_sem.at[n * seqs + s]
            )
            local[ra, ry, s].start()

    def each(body):
        @pl.loop(0, rows // 16)
        def _(i):
            body(pl.ds(i * 16, 16))

    def add_core(ra, ry, s):
        local[ra, ry, s].wait()
        core[ra, ry, s].wait_recv()

        def step(at):
            total = keep[ra, ry, s, at].astype(F32) + from_core[ra, ry, s, at].astype(F32)
            if ra or ry:
                keep[ra, ry, s, at] = total.astype(BF)
            else:
                out[s, at] = total

        each(step)

    base = 4 * seqs
    x_far, y_far, x_near, y_near, x_end, y_end = {}, {}, {}, {}, {}, {}
    for s in range(seqs):
        add_core(1, 1, s)
        x_far[s] = send(keep.at[1, 1, s, :, first], x_in.at[0, s], base + s, x_peer)
        y_far[s] = send(keep.at[1, 1, s, :, second], y_in.at[0, s], base + seqs + s, y_peer)
    for s in range(seqs):
        add_core(1, 0, s)
        x_near[s] = send(keep.at[1, 0, s, :, first], x_in.at[1, s], base + 2 * seqs + s, x_peer)
        add_core(0, 1, s)
        y_near[s] = send(keep.at[0, 1, s, :, second], y_in.at[1, s], base + 3 * seqs + s, y_peer)
    for s in range(seqs):
        add_core(0, 0, s)
    for s in range(seqs):
        x_far[s].wait_recv()

        def step_x(at):
            keep[0, 1, s, at, first] = (
                keep[0, 1, s, at, first].astype(F32) + x_in[0, s, at].astype(F32)
            ).astype(BF)

        each(step_x)
        y_end[s] = send(keep.at[0, 1, s, :, first], y_last.at[s], base + 4 * seqs + s, y_peer)
        y_far[s].wait_recv()

        def step_y(at):
            keep[1, 0, s, at, second] = (
                keep[1, 0, s, at, second].astype(F32) + y_in[0, s, at].astype(F32)
            ).astype(BF)

        each(step_y)
        x_end[s] = send(keep.at[1, 0, s, :, second], x_last.at[s], base + 5 * seqs + s, x_peer)
    for s in range(seqs):
        x_near[s].wait_recv()
        y_near[s].wait_recv()

        def step_near(at):
            out[s, at, first] = out[s, at, first] + x_in[1, s, at].astype(F32)
            out[s, at, second] = out[s, at, second] + y_in[1, s, at].astype(F32)

        each(step_near)
    for s in range(seqs):
        x_end[s].wait_recv()
        y_end[s].wait_recv()

        def step_end(at):
            out[s, at, first] = out[s, at, first] + y_last[s, at].astype(F32)
            out[s, at, second] = out[s, at, second] + x_last[s, at].astype(F32)

        each(step_end)
    for group in (core, x_far, y_far, x_near, y_near, x_end, y_end):
        for copy in group.values():
            copy.wait_send()


def spread(own):
    seqs, rows, width = own.shape
    out = pl.pallas_call(
        spread_kernel,
        out_shape=jax.ShapeDtypeStruct((2, seqs, 4, rows, width), own.dtype),
        in_specs=[pl.BlockSpec(memory_space=pl.ANY)],
        out_specs=pl.BlockSpec(memory_space=pl.ANY),
        scratch_shapes=[
            pltpu.SemaphoreType.DMA,
            pltpu.SemaphoreType.DMA((25,)),
            pltpu.SemaphoreType.DMA((25,)),
        ],
        compiler_params=pltpu.CompilerParams(collective_id=0, has_side_effects=True),
        name="spread",
    )(own)
    return out.reshape(8 * seqs * rows, width)


def row_total(part, seqs):
    tokens, width = part.shape
    rows = tokens // (8 * seqs)
    half = width // 2
    out = pl.pallas_call(
        total_kernel,
        out_shape=jax.ShapeDtypeStruct((seqs, rows, width), F32),
        in_specs=[pl.BlockSpec(memory_space=pl.ANY)],
        out_specs=pl.BlockSpec(memory_space=pltpu.VMEM),
        scratch_shapes=[
            pltpu.VMEM((2, 2, seqs, rows, width), BF),
            pltpu.VMEM((2, 2, seqs, rows, width), BF),
            pltpu.VMEM((2, seqs, rows, half), BF),
            pltpu.VMEM((2, seqs, rows, half), BF),
            pltpu.VMEM((seqs, rows, half), BF),
            pltpu.VMEM((seqs, rows, half), BF),
            pltpu.SemaphoreType.DMA((4 * seqs,)),
            pltpu.SemaphoreType.DMA((10 * seqs,)),
            pltpu.SemaphoreType.DMA((10 * seqs,)),
        ],
        compiler_params=pltpu.CompilerParams(
            collective_id=1, has_side_effects=True, vmem_limit_bytes=32 << 20
        ),
        name="row_total",
    )(part.reshape(2, seqs, 4, rows, width))
    return out.reshape(seqs * rows, width)


def lane_sign(shape):
    return jnp.where(lax.broadcasted_iota(jnp.int32, shape, 1) < HD // 2, -1.0, 1.0)


def score_block(query, key, query_ids, key_ids):
    scores = dot_nt(query, key) * SCALE
    return jnp.where(key_ids > query_ids, NEG_FILL, scores)


def attend_kernel(
    q, k, v, inv, q_gain, k_gain, cosine, sine, column_ids, row_ids, q_out, k_out, att_out, log_out
):
    turn = sine[...] * lane_sign(sine.shape)

    def rotated(pre, column, gain):
        normed = pre[...] * inv[:, column : column + 1] * gain[...]
        return (normed * cosine[...] + pltpu.roll(normed, HD // 2, 1) * turn).astype(BF)

    query, key = rotated(q, 0, q_gain), rotated(k, 1, k_gain)
    scores = score_block(query, key, column_ids[...], row_ids[0])
    top = jnp.max(scores, axis=1, keepdims=True)
    grown = jnp.exp(scores - top)
    total = jnp.sum(grown, axis=1, keepdims=True)
    probs = (grown / total).astype(BF)
    att_out[...] = dot(probs, v[...].astype(BF)).astype(BF)
    q_out[...] = query
    k_out[...] = key
    log_out[0] = top + jnp.log(total)


def attend_back_kernel(
    q, k, v, inv, q_gain, k_gain, cosine, sine, column_ids, row_ids, query, key, grad, log_total,
    q_scaled, k_scaled, v_out, q_dot, k_dot, q_part, k_part,
):
    back = -lane_sign(sine.shape)
    scores = score_block(query[...], key[...], column_ids[...], row_ids[0])
    probs = jnp.exp(scores - log_total[0])
    prob_grad = dot_nt(grad[...], v[...].astype(BF))
    inner = jnp.sum(probs * prob_grad, axis=1, keepdims=True)
    score_grad = (probs * (prob_grad - inner)).astype(BF)
    v_out[...] = dot_tn(probs.astype(BF), grad[...]).astype(BF)

    def finish(rot_grad, pre, column, gain, scaled, dots, parts):
        normed = rot_grad * cosine[...] + pltpu.roll(rot_grad * sine[...], HD // 2, 1) * back
        parts[0] = jnp.sum(normed * pre[...] * inv[:, column : column + 1], axis=0, keepdims=True)
        normed = normed * gain[...]
        scaled[...] = normed
        dots[0] = jnp.sum(normed * pre[...], axis=1, keepdims=True)

    finish(dot(score_grad, key[...]) * SCALE, q, 0, q_gain, q_scaled, q_dot, q_part)
    finish(dot_tn(score_grad, query[...]) * SCALE, k, 1, k_gain, k_scaled, k_dot, k_part)


def attention_specs(length, heads):
    def tile(first):
        return pl.BlockSpec((length, HD), lambda s, h, first=first: (s, first + h))

    table = pl.BlockSpec((length, HD), lambda s, h: (s, 0))
    gain = pl.BlockSpec((1, HD), lambda s, h: (0, h))
    token = pl.BlockSpec((1, length, 1), lambda s, h: (h, s, 0))
    common = [
        tile(0),
        tile(heads),
        tile(2 * heads),
        pl.BlockSpec((length, 2), lambda s, h: (s, 0)),
        gain,
        gain,
        table,
        table,
        pl.BlockSpec((length, 1), lambda s, h: (s, 0)),
        pl.BlockSpec((1, 1, length), lambda s, h: (s, 0, 0)),
    ]
    return tile(0), token, common


def norm_back(source, inv_scale, gain_vec, grad_in):
    scaled = grad_in * gain_vec
    return inv_scale * scaled - source * inv_scale**3 * jnp.mean(
        source * scaled, axis=1, keepdims=True
    )


def body(
    inputs,
    query_weight,
    key_weight,
    value_weight,
    out_weight,
    query_gain,
    key_gain,
    attn_gain,
    gate_weight,
    up_weight,
    down_weight,
    ffn_gain,
    positions,
    block_ids,
    cotangent,
):
    dp = lax.axis_size("dp")
    seqs, rows, _ = inputs.shape
    local = seqs * rows
    tokens = 8 * local
    length = 4 * rows
    hw = query_weight.shape[1] // 2
    heads = hw // HD
    side = lax.axis_index("dp") % 2

    x_perm = [(i, i ^ 1) for i in range(dp)]
    y_perm = [(i, i ^ 2) for i in range(4)]
    c_perm = [(i, i ^ 1) for i in range(4)]
    z_groups = [list(range(0, dp, 2)), list(range(1, dp, 2))]

    def x_send(array):
        return lax.ppermute(array, "dp", x_perm)

    def y_send(array):
        return lax.ppermute(array, "tensor", y_perm)

    def core_send(array):
        return lax.ppermute(array, "tensor", c_perm)

    def by_side(mine, other, axis):
        return jnp.concatenate(
            [jnp.where(side == 0, mine, other), jnp.where(side == 0, other, mine)], axis=axis
        )

    def column_half(array, which):
        width = array.shape[-1] // 2
        return lax.dynamic_slice_in_dim(array, which * width, width, array.ndim - 1)

    def pair_rows(*weights):
        mine = jnp.concatenate([column_half(w, side) for w in weights], axis=1)
        theirs = jnp.concatenate([column_half(w, 1 - side) for w in weights], axis=1)
        return mine, x_send(theirs)

    def gather(*weights):
        mine, other = pair_rows(*weights)
        return lax.all_gather(
            by_side(mine, other, 0), "dp", axis=0, tiled=True, axis_index_groups=z_groups
        )

    def reduce_grad(features, grads):
        summed = lax.psum_scatter(
            dot_tn(features, grads).astype(BF),
            "dp",
            scatter_dimension=0,
            tiled=True,
            axis_index_groups=z_groups,
        )
        width = summed.shape[0] // 2
        mine = lax.dynamic_slice_in_dim(summed, side * width, width, 0)
        theirs = lax.dynamic_slice_in_dim(summed, (1 - side) * width, width, 0)
        return mine, x_send(theirs)

    def sum_rows(vectors):
        parts = lax.psum(vectors.reshape(-1, HD), "tensor")
        return (parts + x_send(parts)).reshape(vectors.shape)

    qkv_w = gather(query_weight, key_weight, value_weight)
    out_w = gather(out_weight)
    gate_w = gather(gate_weight)
    up_w = gather(up_weight)
    down_w = gather(down_weight)
    own_tokens = inputs.reshape(local, D)
    tok_full = spread(inputs)
    attn_g, ffn_g = attn_gain[None], ffn_gain[None]
    query_g, key_g = column_half(query_gain[None], side), column_half(key_gain[None], side)
    cot_rows = cotangent.reshape(local, D)

    pre = dot(tok_full, qkv_w)
    query_pre, key_pre = pre[:, :hw], pre[:, hw : 2 * hw]
    squares = sum_rows(
        jnp.stack([jnp.sum(query_pre * query_pre, axis=1), jnp.sum(key_pre * key_pre, axis=1)])
    )
    inverses = lax.rsqrt(squares / D + EPS)
    query_inv, key_inv = inverses[0][:, None], inverses[1][:, None]
    marks = jnp.stack([positions, block_ids])
    marks = by_side(marks, x_send(marks), 1)
    cosine, sine = rope_tables(marks[0].reshape(tokens))
    tile, token, common = attention_specs(length, heads)
    wide = jax.ShapeDtypeStruct((tokens, hw), BF)
    narrow = jax.ShapeDtypeStruct((heads, tokens, 1), F32)
    attention_args = (
        pre, pre, pre, inverses.T, query_g, key_g, cosine, sine,
        marks[1].reshape(tokens, 1), marks[1].reshape(2 * seqs, 1, length),
    )
    query_rot, key_rot, attended, log_total = pl.pallas_call(
        attend_kernel,
        grid=(2 * seqs, heads),
        out_shape=(wide, wide, wide, narrow),
        in_specs=common,
        out_specs=(tile, tile, tile, token),
        compiler_params=pltpu.CompilerParams(vmem_limit_bytes=32 << 20),
        name="attend",
    )(*attention_args)
    attn_rows = row_total(dot_nt(attended, out_w).astype(BF), seqs)
    attn_inv = lax.rsqrt(jnp.mean(attn_rows * attn_rows, axis=1, keepdims=True) + EPS)
    hidden_rows = own_tokens.astype(F32) + attn_rows * attn_inv * attn_g
    mid_full = spread(hidden_rows.astype(BF).reshape(inputs.shape))
    gate_pre = dot(mid_full, gate_w)
    up_pre = dot(mid_full, up_w)
    gate_sig = jax.nn.sigmoid(gate_pre)
    mixed = (gate_pre * gate_sig * up_pre).astype(BF)
    ffn_rows = row_total(dot_nt(mixed, down_w).astype(BF), seqs)
    ffn_inv = lax.rsqrt(jnp.mean(ffn_rows * ffn_rows, axis=1, keepdims=True) + EPS)
    output_rows = hidden_rows + ffn_rows * ffn_inv * ffn_g

    ffn_back = norm_back(ffn_rows, ffn_inv, ffn_g, cot_rows)
    ffn_gain_part = jnp.sum(cot_rows * ffn_rows * ffn_inv, axis=0)
    ffn_back_full = spread(ffn_back.astype(BF).reshape(inputs.shape))
    down_grad = reduce_grad(ffn_back_full, mixed)
    mixed_grad = dot(ffn_back_full, down_w)
    gate_low = (mixed_grad * up_pre * gate_sig * (1.0 + gate_pre * (1.0 - gate_sig))).astype(BF)
    up_low = (mixed_grad * gate_pre * gate_sig).astype(BF)
    gate_grad = reduce_grad(mid_full, gate_low)
    up_grad = reduce_grad(mid_full, up_low)
    mid_part = (dot_nt(gate_low, gate_w) + dot_nt(up_low, up_w)).astype(BF)
    hidden_grad = cot_rows + row_total(mid_part, seqs)
    attn_back = norm_back(attn_rows, attn_inv, attn_g, hidden_grad)
    attn_gain_part = jnp.sum(hidden_grad * attn_rows * attn_inv, axis=0)
    attn_back_full = spread(attn_back.astype(BF).reshape(inputs.shape))
    out_grad = reduce_grad(attn_back_full, attended)
    attended_grad = dot(attn_back_full, out_w).astype(BF)
    scaled_out = jax.ShapeDtypeStruct((tokens, hw), F32)
    gain_out = jax.ShapeDtypeStruct((2 * seqs, 1, hw), F32)
    gain_tile = pl.BlockSpec((1, 1, HD), lambda s, h: (s, 0, h))
    query_scaled, key_scaled, value_back, query_dots, key_dots, query_parts, key_parts = (
        pl.pallas_call(
            attend_back_kernel,
            grid=(2 * seqs, heads),
            out_shape=(scaled_out, scaled_out, wide, narrow, narrow, gain_out, gain_out),
            in_specs=common + [tile, tile, tile, token],
            out_specs=(tile, tile, tile, token, token, gain_tile, gain_tile),
            compiler_params=pltpu.CompilerParams(vmem_limit_bytes=32 << 20),
            name="attend_back",
        )(*attention_args, query_rot, key_rot, attended_grad, log_total)
    )
    query_gain_part = jnp.sum(query_parts, axis=(0, 1))
    key_gain_part = jnp.sum(key_parts, axis=(0, 1))
    dots = sum_rows(
        jnp.stack([jnp.sum(query_dots, axis=(0, 2)), jnp.sum(key_dots, axis=(0, 2))])
    )
    query_dot, key_dot = dots[0][:, None], dots[1][:, None]
    query_low = (query_inv * query_scaled - query_pre * query_inv**3 * (query_dot / D)).astype(BF)
    key_low = (key_inv * key_scaled - key_pre * key_inv**3 * (key_dot / D)).astype(BF)
    qkv_low = jnp.concatenate([query_low, key_low, value_back], axis=1)
    qkv_grad = reduce_grad(tok_full, qkv_low)
    input_rows = hidden_grad + row_total(dot_nt(qkv_low, qkv_w).astype(BF), seqs)

    def own_columns(grad):
        return by_side(grad[0], grad[1], 1).astype(F32)

    def own_thirds(grad, which):
        return own_columns([part[:, which * hw : (which + 1) * hw] for part in grad])

    def sum_dp(array):
        step = 1
        while step < dp:
            array = array + lax.ppermute(array, "dp", [(i, i ^ step) for i in range(dp)])
            step *= 2
        return array

    def placed(part):
        return lax.dynamic_update_slice(jnp.zeros((2 * hw,), F32), part, (side * hw,))

    shared = jnp.stack([attn_gain_part, ffn_gain_part])
    shared = shared + core_send(shared)
    shared = shared + y_send(shared)
    gains = sum_dp(
        jnp.concatenate(
            [placed(query_gain_part), placed(key_gain_part), shared.reshape(-1)]
        ).reshape(-1, HD)
    ).reshape(-1)
    return (
        output_rows.astype(BF).reshape(inputs.shape),
        input_rows.reshape(inputs.shape),
        own_thirds(qkv_grad, 0),
        own_thirds(qkv_grad, 1),
        own_thirds(qkv_grad, 2),
        own_columns(out_grad),
        gains[: 2 * hw],
        gains[2 * hw : 4 * hw],
        gains[4 * hw : 4 * hw + D],
        own_columns(gate_grad),
        own_columns(up_grad),
        own_columns(down_grad),
        gains[4 * hw + D :],
    )


def solution(mesh):
    whole = P()
    both = P("dp", "tensor")
    rows = P("dp", "tensor", None)
    lanes = P("tensor")
    return jax.shard_map(
        body,
        mesh=mesh,
        in_specs=(
            rows, both, both, both, both, lanes, lanes, whole, both, both, both, whole,
            P("dp", None), P("dp", None), rows,
        ),
        out_specs=(
            rows, rows, both, both, both, both, lanes, lanes, whole, both, both, both, whole,
        ),
        check_vma=False,
    )
```

time: 1140 us -> 1010 us (0.89)
  Pallas kernels: 0 us -> 347 us
  other arithmetic: 238 us -> 44.7 us
  local copies, waits for them, and re-layouts: 160 us -> 41.9 us
  waiting for transfers between devices: 407 us -> 327 us
  matrix products: 225 us -> 184 us
  starting transfers between devices: 56.4 us -> 22.8 us
    pallas_call x0 -> x10, Pallas kernels: none -> 347 us  [the longest x4 162 us: spread(): pl.pallas_call(spread_kernel, out_shape=jax.ShapeDtypeStruct((2, seqs, 4,...]
    reduce_scatter x5, waiting for transfers between devices: 0.03 us -> 180 us  [reduce_grad(): lax.psum_scatter(dot_tn(features, grads).astype(BF), 'dp', scatter_dimens...]
    ppermute x29 -> x13, waiting for transfers between devices: 192 us -> 53.5 us  [x_send(): return lax.ppermute(array, 'dp', x_perm)]
    concatenate x22 -> x0, other arithmetic: 138 us -> none  [the longest x4 121 us: spread(): even = jnp.concatenate([low, high], axis=1)]
    ppermute x17 -> x1, waiting for transfers between devices: 115 us -> 2.17 us  [y_send(): return lax.ppermute(array, 'tensor', y_perm)]
    unnamed x214 -> x117, local copies, waits for them, and re-layouts: 71.3 us -> 26.9 us
    dot_general x5 -> x0, matrix products: 23.5 us -> none  [the longest x1 5.65 us: body(): jnp.einsum('shqk,shqd->shkd', probs_low, attended_grad, preferred_element...]
    reshape x13 -> x2, local copies, waits for them, and re-layouts: 22.8 us -> 0.03 us  [sum_rows(): parts = lax.psum(vectors.reshape(-1, HD), 'tensor')]
  transfers between devices with their start and end apart: 68 -> 28, of which waited for: 37 -> 17; matrix products, arithmetic and copies ran while one was open for 41% -> 15% of each run, Pallas kernels for 0% -> 17%
where the time goes in v3:
time: 1010 us
  Pallas kernels  347 us (34%)
  waiting for transfers between devices  327 us (32%)
  matrix products  184 us (18%)
  other arithmetic  44.7 us (4%)
  local copies, waits for them, and re-layouts  41.9 us (4%)
  blocking collectives  22.9 us (2%)
  starting transfers between devices  22.8 us (2%)
  between operations  15.6 us (2%)
    reduce_scatter x5, waiting for transfers between devices, reduce_grad(): lax.psum_scatter(dot_tn(features, grads).astype(BF), 'dp', scatter_dimens...  180 us
    pallas_call x4, Pallas kernels, spread(): pl.pallas_call(spread_kernel, out_shape=jax.ShapeDtypeStruct((2, seqs, 4,...  162 us
    pallas_call x4, Pallas kernels, row_total(): pl.pallas_call(total_kernel, out_shape=jax.ShapeDtypeStruct((seqs, rows,...  155 us
    all_gather x5, waiting for transfers between devices, gather(): lax.all_gather(by_side(mine, other, 0), 'dp', axis=0, tiled=True, axis_in...  83.5 us
    dot_general x5, matrix products, dot(): return jnp.dot(left, right, preferred_element_type=F32)  67.6 us
    dot_general x5, matrix products, dot_tn(): lax.dot_general(left, right, (((0,), (0,)), ((), ())), preferred_element_...  59.5 us
    dot_general x5, matrix products, dot_nt(): lax.dot_general(left, right, (((1,), (1,)), ((), ())), preferred_element_...  56.8 us
    ppermute x13, waiting for transfers between devices, x_send(): return lax.ppermute(array, 'dp', x_perm)  53.5 us
  transfers between devices with their start and end apart: 28, of which 17 were waited for; matrix products, arithmetic and copies ran while one was open for 15% of the time, Pallas kernels for 17%

profile of v3, /device:TPU:0, one launch (start us, length us, event | category | flops | bytes accessed | tf_op | source)
XLA Modules:
  0.0 1005.5 jit_solution(7153592483391068409)
XLA Ops:
  13.4 9.1 collective-permute-done
  31.5 10.2 %collective-permute-done.4 = bf16[256,1024]{1,0:T(8,128)(2,1)S(1)} collective-permute-done((bf16[256,1024]{1,0:T(8,128)(2,1)S(1)}, bf16[256,1024]{1,0:T(8,128)(2,1)S(1)}, u32[]{:S(2)}, u32[]{:S(2)}) %collective-permute-start.4) | collective-permute-done | bytes 524320 | tf_op jit(solution)/shard_map/ppermute | solution.py:384
  44.7 9.7 collective-permute-done.5
  58.8 44.9 %spread.4 = bf16[2,2,4,128,2048]{4,3,2,1,0:T(8,128)(2,1)} custom-call(bf16[2,128,2048]{2,1,0:T(8,128)(2,1)} %own.1), custom_call_target="tpu_custom_call" | custom-call | tf_op jit(solution)/shard_map/spread/pallas_call | solution.py:226
  111.9 10.0 convolution_bitcast_fusion.q.k.v
  125.1 11.9 %psum.14 = f32[32,128]{1,0:T(8,128)S(1)} all-reduce(f32[32,128]{1,0:T(8,128)S(1)} %reshape.293), channel_id=1, replica_groups=mesh['dp'=8,'tensor'=4] {'tensor'}, use_global_device_ids=true, to_apply=%region_2.3 | all-reduce | flops 4096 | bytes 32768 | tf_op jit(solution)/shard_map/psum | solution.py:426
  146.2 12.6 %attend.1 = (bf16[2048,256]{1,0:T(8,128)(2,1)S(1)}, bf16[2048,256]{1,0:T(8,128)(2,1)S(1)}, bf16[2048,256]{1,0:T(8,128)(2,1)S(1)}, f32[2,2048,1]{2,1,0:T(8,128)S(1)}) custom-call(f32[2048,768]{1,0:T(8,128)S(1)} %copy-done.1, f32[2048,768]{1,0:T(8,128)S(1)} %copy-done.1, f32[2048,768]{1,0:T(8,128)S(1)} %copy-done.1, f32[2048,2]{1,0:T(8,128)S(1)} %bitcast.82, ...), custom_call_target="tpu_custom_call" | custom-call | tf_op jit(solution)/shard_map/attend/pallas_call | solution.py:457
  167.1 38.0 %row_total.4 = f32[2,128,2048]{2,1,0:T(8,128)S(1)} custom-call(bf16[2,2,4,128,2048]{4,3,2,1,0:T(8,128)(2,1)S(1)} %bitcast.81), custom_call_target="tpu_custom_call" | custom-call | tf_op jit(solution)/shard_map/row_total/pallas_call | solution.py:246
  206.7 39.7 %spread.5 = bf16[2,2,4,128,2048]{4,3,2,1,0:T(8,128)(2,1)} custom-call(bf16[2,128,2048]{2,1,0:T(8,128)(2,1)} %fusion.1.own), custom_call_target="tpu_custom_call" | custom-call | tf_op jit(solution)/shard_map/spread/pallas_call | solution.py:226
  246.9 14.5 %fusion.12 = f32[2048,1024]{1,0:T(8,128)} fusion(bf16[2048,2048]{1,0:T(8,128)(2,1)} %bitcast.96, bf16[2048,1024]{1,0:T(8,128)(2,1)} %all-gather.10.cloned.1.call-done), kind=kOutput, calls=%fused_computation.127 | convolution fusion | flops 8589934592 | bytes 20971520 | tf_op jit(solution)/shard_map/dot_general | solution.py:18
  261.5 19.8 %all-gather.12.cloned.1.call-done = bf16[2048,1024]{1,0:T(8,128)(2,1)} async-done(((bf16[512,1024]{1,0:T(8,128)(2,1)}), bf16[2048,1024]{1,0:T(8,128)(2,1)}) %all-gather.12.cloned.1.call-update) | async-done | bytes 4194320 | tf_op jit(solution)/shard_map/all_gather | solution.py:408
  281.3 17.0 %multiply_convert_fusion.2 = (bf16[2048,1024]{1,0:T(8,128)(2,1)}, f32[2048,1024]{1,0:T(8,128)}) fusion(f32[2048,1024]{1,0:T(8,128)} %fusion.12, bf16[2048,2048]{1,0:T(8,128)(2,1)} %bitcast.97, bf16[2048,1024]{1,0:T(8,128)(2,1)} %all-gather.12.cloned.1.call-done), kind=kOutput, calls=%fused_computation.3 | convolution fusion | flops 8602517504 | bytes 33554432 | tf_op jit(solution)/shard_map/dot_general | solution.py:18
  298.2 63.8 %all-gather.14.cloned.1.call-done = bf16[2048,1024]{1,0:T(8,128)(2,1)} async-done(((bf16[512,1024]{1,0:T(8,128)(2,1)}), bf16[2048,1024]{1,0:T(8,128)(2,1)}) %all-gather.14.cloned.1.call-update) | async-done | bytes 4194320 | tf_op jit(solution)/shard_map/all_gather | solution.py:408
  362.0 12.2 %convolution_convert_fusion.1 = bf16[2048,2048]{1,0:T(8,128)(2,1)S(1)} fusion(bf16[2048,1024]{1,0:T(8,128)(2,1)} %get-tuple-element.126, bf16[2048,1024]{1,0:T(8,128)(2,1)} %all-gather.14.cloned.1.call-done), kind=kOutput, calls=%fused_computation.6 | convolution fusion | flops 8594128896 | bytes 16777216 | tf_op jit(solution)/shard_map/dot_general | solution.py:22
  374.2 39.6 %row_total.5 = f32[2,128,2048]{2,1,0:T(8,128)S(1)} custom-call(bf16[2,2,4,128,2048]{4,3,2,1,0:T(8,128)(2,1)S(1)} %bitcast.86), custom_call_target="tpu_custom_call" | custom-call | tf_op jit(solution)/shard_map/row_total/pallas_call | solution.py:246
  416.8 39.1 %spread.6 = bf16[2,2,4,128,2048]{4,3,2,1,0:T(8,128)(2,1)} custom-call(bf16[2,128,2048]{2,1,0:T(8,128)(2,1)} %subtract_convert_fusion.3.own), custom_call_target="tpu_custom_call" | custom-call | tf_op jit(solution)/shard_map/spread/pallas_call | solution.py:226
  455.9 20.1 %multiply_convert_fusion.1 = (bf16[2048,1024]{1,0:T(8,128)(2,1)}, bf16[2048,1024]{1,0:T(8,128)(2,1)}) fusion(f32[2048,1024]{1,0:T(8,128)} %fusion.12, f32[2048,1024]{1,0:T(8,128)} %get-tuple-element.127, bf16[2048,2048]{1,0:T(8,128)(2,1)} %bitcast.100, bf16[2048,1024]{1,0:T(8,128)(2,1)} %all-gather.14.cloned.1.call-done), kind=kOutput, calls=%fused_computation.2 | convolution fusion | flops 8617197568 | bytes 37748736 | tf_op jit(solution)/shard_map/dot_general | solution.py:18
  476.0 15.8 %fusion.13 = f32[2048,2048]{1,0:T(8,128)} fusion(bf16[2048,1024]{1,0:T(8,128)(2,1)} %get-tuple-element.69, bf16[2048,1024]{1,0:T(8,128)(2,1)} %all-gather.12.cloned.1.call-done), kind=kOutput, calls=%fused_computation.128 | convolution fusion | flops 8589934592 | bytes 25165824 | tf_op jit(solution)/shard_map/dot_general | solution.py:22
  491.8 15.9 %add_convert_fusion = bf16[2048,2048]{1,0:T(8,128)(2,1)} fusion(f32[2048,2048]{1,0:T(8,128)} %fusion.13, bf16[2048,1024]{1,0:T(8,128)(2,1)} %get-tuple-element.68, bf16[2048,1024]{1,0:T(8,128)(2,1)S(1)} %copy-done.54), kind=kOutput, calls=%fused_computation | convolution fusion | flops 8598323200 | bytes 33554432 | tf_op jit(solution)/shard_map/dot_general | solution.py:22
  511.1 39.4 %row_total.6 = f32[2,128,2048]{2,1,0:T(8,128)S(1)} custom-call(bf16[2,2,4,128,2048]{4,3,2,1,0:T(8,128)(2,1)S(1)} %bitcast.85), custom_call_target="tpu_custom_call" | custom-call | tf_op jit(solution)/shard_map/row_total/pallas_call | solution.py:246
  555.0 38.7 %spread.7 = bf16[2,2,4,128,2048]{4,3,2,1,0:T(8,128)(2,1)} custom-call(bf16[2,128,2048]{2,1,0:T(8,128)(2,1)} %get-tuple-element.72.own), custom_call_target="tpu_custom_call" | custom-call | tf_op jit(solution)/shard_map/spread/pallas_call | solution.py:226
  599.9 16.7 %attend_back.1 = (f32[2048,256]{1,0:T(8,128)S(1)}, f32[2048,256]{1,0:T(8,128)S(1)}, bf16[2048,256]{1,0:T(8,128)(2,1)S(1)}, f32[2,2048,1]{2,1,0:T(8,128)S(1)}, f3...) custom-call(f32[2048,768]{1,0:T(8,128)} %copy-done, f32[2048,768]{1,0:T(8,128)} %copy-done, ...), custom_call_target="tpu_custom_call" | custom-call | tf_op jit(solution)/shard_map/attend_back/pallas_call | solution.py:498
  625.4 11.0 %psum.15 = f32[32,128]{1,0:T(8,128)S(1)} all-reduce(f32[32,128]{1,0:T(8,128)S(1)} %reshape.300), channel_id=1, replica_groups=mesh['dp'=8,'tensor'=4] {'tensor'}, use_global_device_ids=true, to_apply=%region_9.10 | all-reduce | flops 4096 | bytes 32768 | tf_op jit(solution)/shard_map/psum | solution.py:426
  646.1 10.6 %fusion = bf16[2048,768]{0,1:T(8,128)(2,1)} fusion(bf16[2048,2048]{1,0:T(8,128)(2,1)} %bitcast.95, bf16[2048,256]{1,0:T(8,128)(2,1)S(1)} %copy-done.23, bf16[2048,256]{1,0:T(8,128)(2,1)S(1)} %get-tuple-element.71, bf16[2048,256]{1,0:T(8,128)(2,1)S(1)} %get-tuple-element.70), kind=kOutput, calls=%fused_computation.14 | convolution fusion | flops 6453460992 | bytes 14680064 | tf_op jit(solution)/shard_map/dot_general | solution.py:26
  663.8 14.1 %convolution_convert_fusion.3 = bf16[2048,1024]{1,0:T(8,128)(2,1)} fusion(bf16[2048,2048]{1,0:T(8,128)(2,1)} %bitcast.101, bf16[2048,1024]{1,0:T(8,128)(2,1)} %get-tuple-element.126), kind=kOutput, calls=%fused_computation.9 | convolution fusion | flops 8592031744 | bytes 16777216 | tf_op jit(solution)/shard_map/dot_general | solution.py:26
  677.9 14.0 %convolution_convert_fusion.4 = bf16[2048,1024]{1,0:T(8,128)(2,1)} fusion(bf16[2048,2048]{1,0:T(8,128)(2,1)} %bitcast.98, bf16[2048,1024]{1,0:T(8,128)(2,1)} %get-tuple-element.69), kind=kOutput, calls=%fused_computation.10 | convolution fusion | flops 8592031744 | bytes 16777216 | tf_op jit(solution)/shard_map/dot_general | solution.py:26
  692.3 14.1 %convolution_convert_fusion.5 = bf16[2048,1024]{1,0:T(8,128)(2,1)} fusion(bf16[2048,2048]{1,0:T(8,128)(2,1)} %bitcast.99, bf16[2048,1024]{1,0:T(8,128)(2,1)} %get-tuple-element.68), kind=kOutput, calls=%fused_computation.11 | convolution fusion | flops 8592031744 | bytes 16777216 | tf_op jit(solution)/shard_map/dot_general | solution.py:26
  730.3 38.5 %row_total.7 = f32[2,128,2048]{2,1,0:T(8,128)S(1)} custom-call(bf16[2,2,4,128,2048]{4,3,2,1,0:T(8,128)(2,1)S(1)} %bitcast.84), custom_call_target="tpu_custom_call" | custom-call | tf_op jit(solution)/shard_map/row_total/pallas_call | solution.py:246
  775.8 10.2 %collective-permute-done.9 = bf16[256,256]{0,1:T(8,128)(2,1)S(1)} collective-permute-done((bf16[256,256]{0,1:T(8,128)(2,1)S(1)}, bf16[256,256]{0,1:T(8,128)(2,1)S(1)}, u32[]{:S(2)}, u32[]{:S(2)}) %collective-permute-start.9) | collective-permute-done | bytes 131104 | tf_op jit(solution)/shard_map/ppermute | solution.py:384
  788.2 34.2 %reduce-scatter.14.cloned.1.call-done = bf16[512,1024]{1,0:T(8,128)(2,1)} async-done(((bf16[2048,1024]{1,0:T(8,128)(2,1)}), bf16[512,1024]{1,0:T(8,128)(2,1)}) %reduce-scatter.14.cloned.1.call-update) | async-done | bytes 1048592 | tf_op jit(solution)/shard_map/reduce_scatter | solution.py:413
  825.7 76.3 %reduce-scatter.12.cloned.1.call-done = bf16[512,1024]{1,0:T(8,128)(2,1)} async-done(((bf16[2048,1024]{1,0:T(8,128)(2,1)}), bf16[512,1024]{1,0:T(8,128)(2,1)}) %reduce-scatter.12.cloned.1.call-update) | async-done | bytes 1048592 | tf_op jit(solution)/shard_map/reduce_scatter | solution.py:413
  912.5 69.1 %reduce-scatter.10.cloned.1.call-done = bf16[512,1024]{1,0:T(8,128)(2,1)} async-done(((bf16[2048,1024]{1,0:T(8,128)(2,1)}), bf16[512,1024]{1,0:T(8,128)(2,1)}) %reduce-scatter.10.cloned.1.call-update) | async-done | bytes 1048592 | tf_op jit(solution)/shard_map/reduce_scatter | solution.py:413
  (264 shorter events, 159.3 us)
Async XLA Ops:
  7.2 104.7 %all-gather.6.cloned.1.call-start = ((), (), s32[]{:S(2)}) async-start(), calls=%async_computation.5 | async-start | bytes 3932160 | tf_op jit(solution)/shard_map/all_gather | solution.py:408
  10.4 12.1 %collective-permute-start = (bf16[256,768]{1,0:T(8,128)(2,1)S(1)}, bf16[256,768]{1,0:T(8,128)(2,1)S(1)}, u32[]{:S(2)}, u32[]{:S(2)}) collective-permute-start(bf16[256,768]{1,0:T(8,128)(2,1)S(1)} %pad_maximum_fusion.9), channel_id=1, source_target_pairs={{0,4},{4,0},{8,12},{12,8},{16,20},{20,16},{24,28},{28,24},{1,5},{5... | collective-permute-start | bytes 1179656 | tf_op jit(solution)/shard_map/ppermute | solution.py:384
  23.6 139.6 %all-gather.8.cloned.1.call-start = ((), (), s32[]{:S(2)}) async-start(), calls=%async_computation.6 | async-start | bytes 1310720 | tf_op jit(solution)/shard_map/all_gather | solution.py:408
  23.8 5.0 collective-permute-start.3
  29.6 217.3 %all-gather.10.cloned.1.call-start = ((), (), s32[]{:S(2)}) async-start(), calls=%async_computation.7 | async-start | bytes 5242880 | tf_op jit(solution)/shard_map/all_gather | solution.py:408
  29.7 12.0 %collective-permute-start.4 = (bf16[256,1024]{1,0:T(8,128)(2,1)S(1)}, bf16[256,1024]{1,0:T(8,128)(2,1)S(1)}, u32[]{:S(2)}, u32[]{:S(2)}) collective-permute-start(bf16[256,1024]{1,0:T(8,128)(2,1)S(1)} %constant_dynamic-slice_fusion.7), channel_id=1, source_target_pairs={{0,4},{4,0},{8,12},{12,8},{16,20},{20,16},{24,28},{28,24},{1,5},{5... | collective-permute-start | bytes 1572872 | tf_op jit(solution)/shard_map/ppermute | solution.py:384
  43.1 238.2 %all-gather.12.cloned.1.call-start = ((), (), s32[]{:S(2)}) async-start(), calls=%async_computation.8 | async-start | bytes 5242880 | tf_op jit(solution)/shard_map/all_gather | solution.py:408
  43.2 11.2 %collective-permute-start.5 = (bf16[256,1024]{1,0:T(8,128)(2,1)S(1)}, bf16[256,1024]{1,0:T(8,128)(2,1)S(1)}, u32[]{:S(2)}, u32[]{:S(2)}) collective-permute-start(bf16[256,1024]{1,0:T(8,128)(2,1)S(1)} %constant_dynamic-slice_fusion.6), channel_id=1, source_target_pairs={{0,4},{4,0},{8,12},{12,8},{16,20},{20,16},{24,28},{28,24},{1,5},{5... | collective-permute-start | bytes 1572872 | tf_op jit(solution)/shard_map/ppermute | solution.py:384
  55.8 306.2 %all-gather.14.cloned.1.call-start = ((), (), s32[]{:S(2)}) async-start(), calls=%async_computation.9 | async-start | bytes 5242880 | tf_op jit(solution)/shard_map/all_gather | solution.py:408
  55.9 48.0 %collective-permute-start.2 = (s32[2,2,512]{2,0,1:T(2,128)S(1)}, s32[2,2,512]{2,0,1:T(2,128)S(1)}, u32[]{:S(2)}, u32[]{:S(2)}) collective-permute-start(s32[2,2,512]{2,0,1:T(2,128)S(1)} %pad_add_fusion.1), channel_id=1, source_target_pairs={{0,4},{4,0},{8,12},{12,8},{16,20},{20,16},{24,28},{28,24},{1,5},{5... | collective-permute-start | bytes 24584 | tf_op jit(solution)/shard_map/ppermute | solution.py:384
  57.9 50.8 %collective-permute-start.6 = (bf16[256,1024]{1,0:T(8,128)(2,1)}, bf16[256,1024]{1,0:T(8,128)(2,1)}, u32[]{:S(2)}, u32[]{:S(2)}) collective-permute-start(bf16[256,1024]{1,0:T(8,128)(2,1)} %constant_dynamic-slice_fusion.5), channel_id=1, source_target_pairs={{0,4},{4,0},{8,12},{12,8},{16,20},{20,16},{24,28},{28,24},{1,5},{5... | collective-permute-start | bytes 1572872 | tf_op jit(solution)/shard_map/ppermute | solution.py:384
  58.8 45.0 %copy-start.53 = (f32[512]{0:T(512)S(1)}, f32[512]{0:T(512)}, u32[]{:S(2)}) copy-start(f32[512]{0:T(512)} %param.21) | copy-start | bytes 6148
  137.1 3.7 collective-permute-start.1
  139.9 630.6 %reduce-scatter.6.cloned.1.call-start = ((), (), s32[]{:S(2)}) async-start(), calls=%async_computation.10 | async-start | bytes 3932160 | tf_op jit(solution)/shard_map/reduce_scatter | solution.py:413
  140.8 105.5 %copy-start.42 = (f32[32,128]{1,0:T(8,128)}, f32[32,128]{1,0:T(8,128)S(1)}, u32[]{:S(2)}) copy-start(f32[32,128]{1,0:T(8,128)S(1)} %add_rsqrt_fusion) | copy-start | bytes 49156
  636.4 3.7 collective-permute-start.7
  656.7 116.8 %reduce-scatter.8.cloned.1.call-start = ((), (), s32[]{:S(2)}) async-start(), calls=%async_computation.11 | async-start | bytes 1310720 | tf_op jit(solution)/shard_map/reduce_scatter | solution.py:413
  663.7 158.7 %reduce-scatter.14.cloned.1.call-start = ((), (), s32[]{:S(2)}) async-start(), calls=%async_computation.14 | async-start | bytes 5242880 | tf_op jit(solution)/shard_map/reduce_scatter | solution.py:413
  677.9 224.1 %reduce-scatter.12.cloned.1.call-start = ((), (), s32[]{:S(2)}) async-start(), calls=%async_computation.13 | async-start | bytes 5242880 | tf_op jit(solution)/shard_map/reduce_scatter | solution.py:413
  692.0 289.6 %reduce-scatter.10.cloned.1.call-start = ((), (), s32[]{:S(2)}) async-start(), calls=%async_computation.12 | async-start | bytes 5242880 | tf_op jit(solution)/shard_map/reduce_scatter | solution.py:413
  707.1 1.2 collective-permute-start.10
  708.4 3.8 collective-permute-start.11
  712.2 3.8 collective-permute-start.12
  716.1 3.8 collective-permute-start.13
  719.9 50.6 %collective-permute-start.14 = (f32[40,128]{1,0:T(8,128)S(1)}, f32[40,128]{1,0:T(8,128)S(1)}, u32[]{:S(2)}, u32[]{:S(2)}) collective-permute-start(f32[40,128]{1,0:T(8,128)S(1)} %fusion.42), channel_id=1, source_target_pairs={{0,16},{4,20},{8,24},{12,28},{16,0},{20,4},{24,8},{28,12},{1,17},{... | collective-permute-start | bytes 61448 | tf_op jit(solution)/shard_map/ppermute | solution.py:529
  771.5 14.5 %collective-permute-start.8 = (bf16[256,768]{0,1:T(8,128)(2,1)S(1)}, bf16[256,768]{0,1:T(8,128)(2,1)S(1)}, u32[]{:S(2)}, u32[]{:S(2)}) collective-permute-start(bf16[256,768]{0,1:T(8,128)(2,1)S(1)} %constant_dynamic-slice_fusion.4), channel_id=1, source_target_pairs={{0,4},{4,0},{8,12},{12,8},{16,20},{20,16},{24,28},{28,24},{1,5},{5... | collective-permute-start | bytes 1179656 | tf_op jit(solution)/shard_map/ppermute | solution.py:384
  774.4 11.6 %collective-permute-start.9 = (bf16[256,256]{0,1:T(8,128)(2,1)S(1)}, bf16[256,256]{0,1:T(8,128)(2,1)S(1)}, u32[]{:S(2)}, u32[]{:S(2)}) collective-permute-start(bf16[256,256]{0,1:T(8,128)(2,1)S(1)} %constant_dynamic-slice_fusion.3), channel_id=1, source_target_pairs={{0,4},{4,0},{8,12},{12,8},{16,20},{20,16},{24,28},{28,24},{1,5},{5... | collective-permute-start | bytes 393224 | tf_op jit(solution)/shard_map/ppermute | solution.py:384
  824.3 159.9 %collective-permute-start.17 = (bf16[256,1024]{1,0:T(8,128)(2,1)}, bf16[256,1024]{1,0:T(8,128)(2,1)S(1)}, u32[]{:S(2)}, u32[]{:S(2)}) collective-permute-start(bf16[256,1024]{1,0:T(8,128)(2,1)} %constant_dynamic-slice_fusion), channel_id=1, source_target_pairs={{0,4},{4,0},{8,12},{12,8},{16,20},{20,16},{24,28},{28,24},{1,5},{5... | collective-permute-start | bytes 1572872 | tf_op jit(solution)/shard_map/ppermute | solution.py:384
  903.9 80.3 %collective-permute-start.16 = (bf16[256,1024]{1,0:T(8,128)(2,1)}, bf16[256,1024]{1,0:T(8,128)(2,1)}, u32[]{:S(2)}, u32[]{:S(2)}) collective-permute-start(bf16[256,1024]{1,0:T(8,128)(2,1)} %constant_dynamic-slice_fusion.1), channel_id=1, source_target_pairs={{0,4},{4,0},{8,12},{12,8},{16,20},{20,16},{24,28},{28,24},{1,5},{5... | collective-permute-start | bytes 1572872 | tf_op jit(solution)/shard_map/ppermute | solution.py:384
  905.3 78.8 %copy-start.35 = (bf16[512,1024]{1,0:T(8,128)(2,1)S(1)}, bf16[512,1024]{1,0:T(8,128)(2,1)}, u32[]{:S(2)}) copy-start(bf16[512,1024]{1,0:T(8,128)(2,1)} %reduce-scatter.14.cloned.1.call-done) | copy-start | bytes 3145732
  905.3 78.8 %copy-start.36 = (bf16[512,1024]{1,0:T(8,128)(2,1)S(1)}, bf16[512,1024]{1,0:T(8,128)(2,1)}, u32[]{:S(2)}) copy-start(bf16[512,1024]{1,0:T(8,128)(2,1)} %reduce-scatter.12.cloned.1.call-done) | copy-start | bytes 3145732
  982.6 13.8 %collective-permute-start.15 = (bf16[256,1024]{1,0:T(8,128)(2,1)S(1)}, bf16[256,1024]{1,0:T(8,128)(2,1)S(1)}, u32[]{:S(2)}, u32[]{:S(2)}) collective-permute-start(bf16[256,1024]{1,0:T(8,128)(2,1)S(1)} %constant_dynamic-slice_fusion.2), channel_id=1, source_target_pairs={{0,4},{4,0},{8,12},{12,8},{16,20},{20,16},{24,28},{28,24},{1,5},{5... | collective-permute-start | bytes 1572872 | tf_op jit(solution)/shard_map/ppermute | solution.py:384
  (51 other events, 690.0 us)
Sparse Core Ops, SparseCore 0:
  23.7 64.9 all-gather.5
  90.9 26.5 all-gather.7
  119.6 80.2 all-gather.9
  201.9 79.2 all-gather.11
  282.7 79.2 all-gather.13
  656.8 58.1 reduce-scatter.5
  717.3 27.1 reduce-scatter.7
  746.9 75.4 reduce-scatter.13
  824.7 77.2 reduce-scatter.11
  904.3 77.2 reduce-scatter.9
